TPU v7x, 256 devices: a whole 4x4x8 slice. The times are simulated.
256 devices in a mesh: px: 32 (over y, z), py: 8 (over x, core).
Axes of the slice: x: 4, y: 4, z: 8, core: 2. Of those that a mesh axis runs over, the one named last changes fastest.
Arguments:
- eta_boxes: float32 [1024, 32, 32, 128], P(('px', 'py')), may hold values from 0 to 1
- corners: int32 [1024, 2], P(('px', 'py')), may hold values from 0 to 95, as said below
- grain_ids: int32 [1024], P(('px', 'py')), may hold values from 0 to 23
- misfit: float32 [24], replicated, may hold values from -1 to 1
- green: float32 [128, 768, 512], P('px', 'py'), may hold values from 0.25 to 2.5
Outputs:
- eta_next: float32 [1024, 32, 32, 128], P(('px', 'py'))
- potential: float32 [768, 512, 128], P('px', 'py')
Inputs may be any that keep to these rules, and one draw needn't show every extreme that they name: Box b lies with device d = b // 4 (px index p = d // 8, py index q = d % 8): 8 corners[b,0] lies in [p * 24, (p + 1) * 24) and 8 corners[b,1] in [q * 64, (q + 1) * 64). Among each device's boxes one has its corner at the last tile grid position of that device's cells in both columns.
All inputs are finite; a program needn't handle non-finite values.
Results may differ from a plain program's by a relative error of at most 0.000075.
Values sent between devices are 32-bit elements; how exact they have to be, the bound alone decides.
A program may use at most 64 MiB of HBM per device.

v0:
```python
import math

import jax
import jax.numpy as jnp
from jax import lax
from jax.sharding import PartitionSpec as P

NX = 768
NY = 512
NZ = 128
BX = 32
BY = 32
STEP = 8


rate_step = 0.2
gradient_coef = 0.1
coupling = 1.5
precise_mode = lax.Precision.HIGHEST


def from_behind(shard, axis, by):
    peers = lax.axis_size(axis)
    return lax.ppermute(shard, axis, [(i, (i + by) % peers) for i in range(peers)])


def in_blocks(shard, dim, peers):
    before, after = (shard.shape[:dim], shard.shape[dim + 1 :])
    return jnp.moveaxis(shard.reshape(*before, peers, -1, *after), dim, 0)


def piece_ends(length, count):
    unit = 8 if length >= 8 * count else 1
    return [length // unit * k // count * unit for k in range(1, count)]


def in_order(parts, dim):
    parts = jnp.moveaxis(parts, 0, dim)
    lengths = parts.shape
    return parts.reshape(*lengths[:dim], lengths[dim] * lengths[dim + 1], *lengths[dim + 2 :])


def cut_exchange(shard, axis, pieces, split_dim, concat_dim):
    parts = in_blocks(shard, split_dim, lax.axis_size(axis))
    widest = max(range(1, max(2, parts.ndim - 1)), key=lambda d: parts.shape[d])
    done = []
    for section in jnp.split(parts, piece_ends(parts.shape[widest], pieces), axis=widest):
        if section.size:
            done.append(lax.all_to_all(section, axis, split_axis=0, concat_axis=0, tiled=True))
    return in_order(jnp.concatenate(done, axis=widest), concat_dim)


def laplace(values):
    padded = jnp.pad(values, ((1, 1), (1, 1), (0, 0)))
    beside_all = padded[2:, 1:-1] + padded[:-2, 1:-1] + padded[1:-1, 2:] + padded[1:-1, :-2]
    beside_all = beside_all + jnp.roll(values, 1, axis=2) + jnp.roll(values, -1, axis=2)
    return beside_all - 6.0 * values


def advance(order_param, weight, field_mu, occupancy):
    square = order_param * order_param
    force = order_param * square - order_param + 2.0 * coupling * order_param * (occupancy - square)
    force = force - gradient_coef * laplace(order_param) + 2.0 * weight * order_param * field_mu
    return order_param - rate_step * force


def spectra(length):
    counter = jnp.arange(length, dtype=jnp.int32)
    phase_index = counter[:, None] * counter[None, :] % length
    angles = phase_index.astype(jnp.float32) * (2.0 * math.pi / length)
    return (jnp.cos(angles), jnp.sin(angles))


def product(pattern, operand, table_mat):
    return jnp.einsum(pattern, operand, table_mat, precision=precise_mode)


def on_device(eta_boxes, corners, grain_ids, misfit, green):
    rows_dev = NX // lax.axis_size("px")
    cols_dev = NY // lax.axis_size("py")
    over_x = BX - STEP
    over_y = BY - STEP
    start_x = corners[:, 0] * STEP - lax.axis_index("px") * rows_dev
    start_y = corners[:, 1] * STEP - lax.axis_index("py") * cols_dev
    variant = jnp.arange(misfit.shape[0], dtype=jnp.int32)
    weights = jnp.sum(
        jnp.where(grain_ids[:, None] == variant[None, :], misfit[None, :], 0.0), axis=1
    )
    squares = eta_boxes * eta_boxes
    anchor_zero = jnp.zeros((), jnp.int32)
    box_count = eta_boxes.shape[0]
    box_patch = jnp.zeros((2, rows_dev + over_x, cols_dev + over_y, NZ), jnp.float32)
    for box_slot in range(box_count):
        contrib = jnp.stack([weights[box_slot] * squares[box_slot], squares[box_slot]])
        position = (anchor_zero, start_x[box_slot], start_y[box_slot], anchor_zero)
        current = lax.dynamic_slice(box_patch, position, contrib.shape)
        box_patch = lax.dynamic_update_slice(box_patch, current + contrib, position)
    beside_x = from_behind(box_patch[:, rows_dev:, :cols_dev], "px", 1)
    beside_y = from_behind(box_patch[:, :rows_dev, cols_dev:], "py", 1)
    first_leg = from_behind(box_patch[:, rows_dev:, cols_dev:], "px", 1)
    diagonal = from_behind(first_leg, "py", 1)
    grid_field = box_patch[:, :rows_dev, :cols_dev]
    grid_field = grid_field.at[:, :over_x].add(beside_x)
    grid_field = grid_field.at[:, :, :over_y].add(beside_y)
    grid_field = grid_field.at[:, :over_x, :over_y].add(diagonal)
    cosine_depth, sine_depth = spectra(NZ)
    cosine_rows, sine_rows = spectra(NX)
    cosine_cols, sine_cols = spectra(NY)
    eigen_field = grid_field[0]
    depth_real = product("xyz,zk->kyx", eigen_field, cosine_depth)
    depth_imag = -product("xyz,zk->kyx", eigen_field, sine_depth)
    pieces = lax.all_to_all(
        jnp.stack([depth_real, depth_imag]), "px", split_axis=1, concat_axis=3, tiled=True
    )
    real_part = product("zyx,xk->zyk", pieces[0], cosine_rows) + product(
        "zyx,xk->zyk", pieces[1], sine_rows
    )
    imag_part = product("zyx,xk->zyk", pieces[1], cosine_rows) - product(
        "zyx,xk->zyk", pieces[0], sine_rows
    )
    along_x = jnp.stack([real_part, imag_part])
    along_y = cut_exchange(along_x, "py", 2, 3, 2)
    spec_real = (
        product("zyx,yk->zxk", along_y[0], cosine_cols)
        + product("zyx,yk->zxk", along_y[1], sine_cols)
    ) * green
    spec_imag = (
        product("zyx,yk->zxk", along_y[1], cosine_cols)
        - product("zyx,yk->zxk", along_y[0], sine_cols)
    ) * green
    back_real = product("zxk,ky->zyx", spec_real, cosine_cols) - product(
        "zxk,ky->zyx", spec_imag, sine_cols
    )
    back_imag = product("zxk,ky->zyx", spec_imag, cosine_cols) + product(
        "zxk,ky->zyx", spec_real, sine_cols
    )
    returned = lax.all_to_all(
        jnp.stack([back_real, back_imag]), "py", split_axis=2, concat_axis=3, tiled=True
    )
    rows_real = product("zyk,kx->zyx", returned[0], cosine_rows) - product(
        "zyk,kx->zyx", returned[1], sine_rows
    )
    rows_imag = product("zyk,kx->zyx", returned[1], cosine_rows) + product(
        "zyk,kx->zyx", returned[0], sine_rows
    )
    inverse_scale = 1.0 / (NX * NY * NZ)
    pieces = lax.all_to_all(
        jnp.stack([rows_real, rows_imag]), "px", split_axis=3, concat_axis=1, tiled=True
    )
    summed = product("kyx,kz->xyz", pieces[0], cosine_depth) - product(
        "kyx,kz->xyz", pieces[1], sine_depth
    )
    potential = summed * inverse_scale
    handed = jnp.stack([potential, grid_field[1]])
    upper_tile = from_behind(handed[:, :, :over_y], "py", -1)
    column_pair = jnp.concatenate([handed, upper_tile], axis=2)
    next_column = from_behind(column_pair, "px", -1)
    window_all = jnp.concatenate([column_pair, next_column], axis=1)
    results = []
    for box_slot in range(box_count):
        position = (anchor_zero, start_x[box_slot], start_y[box_slot], anchor_zero)
        window_vals = lax.dynamic_slice(window_all, position, (2,) + eta_boxes.shape[1:])
        results.append(
            advance(eta_boxes[box_slot], weights[box_slot], window_vals[0], window_vals[1])
        )
    return (jnp.stack(results), potential)


def solution(mesh):
    in_specs = (
        P(("px", "py"), None, None, None),
        P(("px", "py"), None),
        P(("px", "py")),
        P(),
        P("px", "py", None),
    )
    out_specs = (P(("px", "py"), None, None, None), P("px", "py", None))
    return jax.shard_map(
        on_device, mesh=mesh, in_specs=in_specs, out_specs=out_specs, check_vma=False
    )
```

profile of v0, /device:TPU:1, one launch (start us, length us, event | category | flops | bytes accessed | tf_op | source)
XLA Modules:
  0.0 570.7 jit_solution(13513579270630001621)
XLA Ops:
  25.4 6.3 %dynamic_update_slice.12 = f32[2,48,88,128]{3,2,1,0:T(8,128)} dynamic-update-slice(f32[2,48,88,128]{3,2,1,0:T(8,128)} %broadcast_in_dim.14, f32[2,32,32,128]{3,2,1,0:T(8,128)S(1)} %pad_maximum_fusion.6, s32[]{:T(128)} %constant.140.clone.1, s32[]{:T(128)S(6)} %select_n.98, s32[]{:T(128)S(6)} %select_n.99, s32[]{:T(128)} %constant.140.clone.1) | dynamic-update-slice | bytes 2097156 | tf_op jit(solution)/shard_map/dynamic_update_slice | solution.py:97
  42.1 6.4 %dynamic_update_slice.14 = f32[2,48,88,128]{3,2,1,0:T(8,128)} dynamic-update-slice(f32[2,48,88,128]{3,2,1,0:T(8,128)} %dynamic_update_slice.13, f32[2,32,32,128]{3,2,1,0:T(8,128)S(1)} %maximum_add_fusion.1, s32[]{:T(128)} %constant.140.clone.1, s32[]{:T(128)S(6)} %select_n.102, s32[]{:T(128)S(6)} %select_n.103, s32[]{:T(128)} %constant.140.clone.1) | dynamic-update-slice | bytes 2097156 | tf_op jit(solution)/shard_map/dynamic_update_slice | solution.py:97
  66.1 48.5 %collective-permute-done.2 = f32[2,24,24,128]{3,2,1,0:T(8,128)S(1)} collective-permute-done((f32[2,24,24,128]{3,2,1,0:T(8,128)S(1)}, f32[2,24,24,128]{3,2,1,0:T(8,128)S(1)}, u32[]{:S(2)}, u32[]{:S(2)}) %collective-permute-start.2) | collective-permute-done | bytes 589856 | tf_op jit(solution)/shard_map/ppermute | solution.py:24
  132.7 40.9 %all_to_all.55 = f32[32,1,12288]{2,1,0:T(1,128)S(1)} all-to-all(f32[32,1,12288]{2,1,0:T(1,128)} %reshape.165), channel_id=1, replica_groups=mesh['px'=32,'py'=8] {'px'}, dimensions={0} | all-to-all | bytes 3145728 | tf_op jit(solution)/shard_map/all_to_all | solution.py:112
  185.9 14.4 %fusion.8 = f32[4,64,768]{2,1,0:T(8,128)S(1)} fusion(f32[4,64,768]{1,2,0:T(8,128)S(1)} %bitcast.209), kind=kOutput, calls=%fused_computation.10 | convolution fusion | flops 1817247744 | bytes 1572864 | tf_op jit(solution)/shard_map/zyx,xk->zyk/dot_general | solution.py:75
  200.4 16.9 %fusion.6 = f32[4,64,768]{2,1,0:T(8,128)} fusion(f32[4,64,768]{1,2,0:T(8,128)S(1)} %bitcast.211), kind=kOutput, calls=%fused_computation.8 | convolution fusion | flops 1817247744 | bytes 1572864 | tf_op jit(solution)/shard_map/zyx,xk->zyk/dot_general | solution.py:75
  217.4 14.5 %fusion.46 = f32[4,64,768]{2,1,0:T(8,128)S(1)} fusion(f32[4,64,768]{2,1,0:T(8,128)S(1)} %fusion.8, f32[4,64,768]{1,2,0:T(8,128)S(1)} %bitcast.212), kind=kOutput, calls=%fused_computation.54 | convolution fusion | flops 1817444352 | bytes 2359296 | tf_op jit(solution)/shard_map/zyx,xk->zyk/dot_general | solution.py:75
  233.6 15.9 %fusion.49 = f32[4,64,768]{2,1,0:T(8,128)S(1)} fusion(f32[4,64,768]{2,1,0:T(8,128)} %fusion.6, f32[4,64,768]{1,2,0:T(8,128)} %bitcast.210), kind=kOutput, calls=%fused_computation.55 | convolution fusion | flops 1817444352 | bytes 2359296 | tf_op jit(solution)/shard_map/zyx,xk->zyk/dot_general | solution.py:75
  251.6 24.7 %all_to_all.56 = f32[8,2,4,32,96]{4,3,2,1,0:T(8,128)S(1)} all-to-all(f32[8,2,4,32,96]{4,3,2,1,0:T(8,128)S(1)} %get-tuple-element.60), channel_id=1, replica_groups=mesh['px'=32,'py'=8] {'py'}, dimensions={0} | all-to-all | bytes 1572864 | tf_op jit(solution)/shard_map/all_to_all | solution.py:49
  276.3 18.8 %all_to_all.57 = f32[8,2,4,32,96]{4,3,2,1,0:T(8,128)S(1)} all-to-all(f32[8,2,4,32,96]{4,3,2,1,0:T(8,128)S(1)} %get-tuple-element.61), channel_id=1, replica_groups=mesh['px'=32,'py'=8] {'py'}, dimensions={0} | all-to-all | bytes 1572864 | tf_op jit(solution)/shard_map/all_to_all | solution.py:49
  295.6 7.4 %fusion.101 = f32[4,96,512]{2,1,0:T(8,128)S(1)} fusion(f32[4,512,96]{2,1,0:T(8,128)S(1)} %bitcast.213), kind=kOutput, calls=%fused_computation.93 | convolution fusion | flops 1211629568 | bytes 1572864 | tf_op jit(solution)/shard_map/zyx,yk->zxk/dot_general | solution.py:75
  303.1 7.3 %fusion.97 = f32[4,96,512]{2,1,0:T(8,128)S(1)} fusion(f32[4,512,96]{2,1,0:T(8,128)S(1)} %bitcast.215), kind=kOutput, calls=%fused_computation.89 | convolution fusion | flops 1211629568 | bytes 1572864 | tf_op jit(solution)/shard_map/zyx,yk->zxk/dot_general | solution.py:75
  310.4 7.4 %fusion.45 = f32[4,96,512]{2,1,0:T(8,128)S(1)} fusion(f32[4,96,512]{2,1,0:T(8,128)S(1)} %copy-done.8, f32[4,96,512]{2,1,0:T(8,128)S(1)} %fusion.101, f32[4,512,96]{2,1,0:T(8,128)S(1)} %bitcast.216), kind=kOutput, calls=%fused_computation.53 | convolution fusion | flops 1212022784 | bytes 3145728 | tf_op jit(solution)/shard_map/zyx,yk->zxk/dot_general | solution.py:75
  317.8 6.0 %fusion.99 = f32[512,4,96]{0,2,1:T(8,128)S(1)} fusion(f32[4,96,512]{2,1,0:T(8,128)S(1)} %fusion.45), kind=kOutput, calls=%fused_computation.91 | convolution fusion | flops 1211629568 | bytes 1572864 | tf_op jit(solution)/shard_map/zxk,ky->zyx/dot_general | solution.py:75
  323.8 7.4 %fusion.44 = f32[4,96,512]{2,1,0:T(8,128)S(1)} fusion(f32[4,96,512]{2,1,0:T(8,128)S(1)} %copy-done.8, f32[4,96,512]{2,1,0:T(8,128)S(1)} %fusion.97, f32[4,512,96]{2,1,0:T(8,128)S(1)} %bitcast.214), kind=kOutput, calls=%fused_computation.51 | convolution fusion | flops 1212022784 | bytes 3145728 | tf_op jit(solution)/shard_map/zyx,yk->zxk/dot_general | solution.py:75
  350.7 31.1 %all_to_all.58 = f32[2,4,512,96]{3,1,0,2:T(4,128)S(1)} all-to-all(f32[2,4,512,96]{3,1,0,2:T(4,128)} %copy.78), channel_id=1, replica_groups=mesh['px'=32,'py'=8] {'py'}, dimensions={2} | all-to-all | bytes 3145728 | tf_op jit(solution)/shard_map/all_to_all | solution.py:137
  384.3 12.2 %fusion.4 = f32[4,64,768]{2,1,0:T(8,128)} fusion(f32[4,64,768]{2,1,0:T(8,128)S(1)} %squeeze.142), kind=kOutput, calls=%fused_computation.6 | convolution fusion | flops 1817247744 | bytes 1572864 | tf_op jit(solution)/shard_map/zyk,kx->zyx/dot_general | solution.py:75
  398.4 13.1 %fusion.2 = f32[4,64,768]{2,1,0:T(8,128)S(1)} fusion(f32[4,64,768]{2,1,0:T(8,128)} %squeeze.141), kind=kOutput, calls=%fused_computation.4 | convolution fusion | flops 1817247744 | bytes 1572864 | tf_op jit(solution)/shard_map/zyk,kx->zyx/dot_general | solution.py:75
  411.5 11.9 %fusion.55 = f32[1,4,64,768]{3,2,1,0:T(8,128)S(1)} fusion(f32[4,64,768]{2,1,0:T(8,128)S(1)} %copy-done.9, f32[4,64,768]{2,1,0:T(8,128)S(1)} %copy-done.7), kind=kOutput, calls=%fused_computation.57 | convolution fusion | flops 1817444352 | bytes 2359296 | tf_op jit(solution)/shard_map/zyk,kx->zyx/dot_general | solution.py:75
  423.4 11.7 %fusion.61 = f32[1,4,64,768]{3,2,1,0:T(8,128)S(1)} fusion(f32[4,64,768]{2,1,0:T(8,128)S(1)} %fusion.2, f32[4,64,768]{2,1,0:T(8,128)S(1)} %squeeze.142), kind=kOutput, calls=%fused_computation.59 | convolution fusion | flops 1817444352 | bytes 2359296 | tf_op jit(solution)/shard_map/zyk,kx->zyx/dot_general | solution.py:75
  449.4 35.9 %all-to-all-done.4 = f32[32,1,12288]{2,1,0:T(1,128)S(1)} async-done(((f32[32,1,12288]{2,1,0:T(1,128)}), f32[32,1,12288]{2,1,0:T(1,128)S(1)}, u32[]{:S(2)}, u32[]{:S(2)}) %all-to-all-start.4) | async-done | bytes 1572896 | tf_op jit(solution)/shard_map/all_to_all | solution.py:147
  485.2 5.9 %reduce.7 = f32[32,12288]{1,0:T(8,128)} reduce(f32[32,1,12288]{2,1,0:T(1,128)S(1)} %all-to-all-done.4, f32[]{:T(128)} %broadcast.204), dimensions={1}, to_apply=%all_to_all.47.reduce_sub_computation | reduce | bytes 3145732 | tf_op jit(solution)/shard_map/all_to_all | solution.py:147
  504.9 8.0 %collective-permute-done.4 = f32[2,24,24,128]{3,2,1,0:T(8,128)S(1)} collective-permute-done((f32[2,24,24,128]{3,2,1,0:T(8,128)S(1)}, f32[2,24,24,128]{3,2,1,0:T(8,128)S(1)}, u32[]{:S(2)}, u32[]{:S(2)}) %collective-permute-start.4) | collective-permute-done | bytes 589856 | tf_op jit(solution)/shard_map/ppermute | solution.py:24
  521.1 43.0 %collective-permute-done.5 = f32[2,24,88,128]{3,2,1,0:T(8,128)} collective-permute-done((f32[2,24,88,128]{3,2,1,0:T(8,128)}, f32[2,24,88,128]{3,2,1,0:T(8,128)}, u32[]{:S(2)}, u32[]{:S(2)}) %collective-permute-start.5) | collective-permute-done | bytes 2162720 | tf_op jit(solution)/shard_map/ppermute | solution.py:24
  (106 shorter events, 135.7 us)
Async XLA Ops:
  58.5 58.3 %collective-permute-start = (f32[2,24,64,128]{3,2,1,0:T(8,128)S(1)}, f32[2,24,64,128]{3,2,1,0:T(8,128)S(1)}, u32[]{:S(2)}, u32[]{:S(2)}) collective-permute-start(f32[2,24,64,128]{3,2,1,0:T(8,128)S(1)} %slice.436), channel_id=1, source_target_pairs={{0,8},{8,16},{16,24},{24,32},{32,40},{40,48},{48,56},{56,64},{64,7... | collective-permute-start | bytes 4718600 | tf_op jit(solution)/shard_map/ppermute | solution.py:24
  63.1 51.6 %collective-permute-start.2 = (f32[2,24,24,128]{3,2,1,0:T(8,128)S(1)}, f32[2,24,24,128]{3,2,1,0:T(8,128)S(1)}, u32[]{:S(2)}, u32[]{:S(2)}) collective-permute-start(f32[2,24,24,128]{3,2,1,0:T(8,128)S(1)} %get-tuple-element.46), channel_id=1, source_target_pairs={{0,8},{8,16},{16,24},{24,32},{32,40},{40,48},{48,56},{56,64},{64,7... | collective-permute-start | bytes 1769480 | tf_op jit(solution)/shard_map/ppermute | solution.py:24
  64.8 53.8 %collective-permute-start.1 = (f32[2,24,24,128]{3,2,1,0:T(8,128)S(1)}, f32[2,24,24,128]{3,2,1,0:T(8,128)S(1)}, u32[]{:S(2)}, u32[]{:S(2)}) collective-permute-start(f32[2,24,24,128]{3,2,1,0:T(8,128)S(1)} %get-tuple-element.47), channel_id=1, source_target_pairs={{0,1},{1,2},{2,3},{3,4},{4,5},{5,6},{6,7},{7,0},{8,9},{9,10},{10,1... | collective-permute-start | bytes 1769480 | tf_op jit(solution)/shard_map/ppermute | solution.py:24
  114.6 8.9 %collective-permute-start.3 = (f32[2,24,24,128]{3,2,1,0:T(8,128)S(1)}, f32[2,24,24,128]{3,2,1,0:T(8,128)S(1)}, u32[]{:S(2)}, u32[]{:S(2)}) collective-permute-start(f32[2,24,24,128]{3,2,1,0:T(8,128)S(1)} %collective-permute-done.2), channel_id=1, source_target_pairs={{0,1},{1,2},{2,3},{3,4},{4,5},{5,6},{6,7},{7,0},{8,9},{9,10},{10,1... | collective-permute-start | bytes 1769480 | tf_op jit(solution)/shard_map/ppermute | solution.py:24
  185.9 14.4 %copy-start.6 = (f32[1,4,64,32,24]{2,4,3,1,0:T(8,128)}, f32[1,4,64,32,24]{2,4,3,1,0:T(8,128)S(1)}, u32[]{:S(2)}) copy-start(f32[1,4,64,32,24]{2,4,3,1,0:T(8,128)S(1)} %copy.66) | copy-start | bytes 2359300
  249.9 1.2 copy-start.4
  303.1 7.3 %copy-start.8 = (f32[4,96,512]{2,1,0:T(8,128)S(1)}, f32[4,96,512]{2,1,0:T(8,128)}, u32[]{:S(2)}) copy-start(f32[4,96,512]{2,1,0:T(8,128)} %param.17) | copy-start | bytes 2359300
  384.3 12.2 %copy-start.5 = (f32[1,4,64,8,96]{4,2,3,1,0:T(8,128)S(1)}, f32[1,4,64,8,96]{4,2,3,1,0:T(8,128)}, u32[]{:S(2)}) copy-start(f32[1,4,64,8,96]{4,2,3,1,0:T(8,128)} %get-tuple-element.57) | copy-start | bytes 2359300
  398.4 13.1 %copy-start.7 = (f32[4,64,768]{2,1,0:T(8,128)S(1)}, f32[4,64,768]{2,1,0:T(8,128)}, u32[]{:S(2)}) copy-start(f32[4,64,768]{2,1,0:T(8,128)} %squeeze.141) | copy-start | bytes 2359300
  398.4 13.1 %copy-start.9 = (f32[4,64,768]{2,1,0:T(8,128)S(1)}, f32[4,64,768]{2,1,0:T(8,128)}, u32[]{:S(2)}) copy-start(f32[4,64,768]{2,1,0:T(8,128)} %fusion.4) | copy-start | bytes 2359300
  442.9 42.3 %all-to-all-start.4 = ((f32[32,1,12288]{2,1,0:T(1,128)}), f32[32,1,12288]{2,1,0:T(1,128)S(1)}, u32[]{:S(2)}, u32[]{:S(2)}) async-start(f32[32,1,12288]{2,1,0:T(1,128)} %reshape.167), calls=%async_computation.4 | async-start | bytes 3145728 | tf_op jit(solution)/shard_map/all_to_all | solution.py:147
  498.4 2.8 copy-start.1
  501.2 13.2 %copy-start.2 = (f32[128,64,24]{0,1,2:T(8,128)}, f32[128,64,24]{0,1,2:T(8,128)S(1)}, u32[]{:S(2)}) copy-start(f32[128,64,24]{0,1,2:T(8,128)S(1)} %fusion.41) | copy-start | bytes 2359300
  501.3 18.1 %copy-start = (f32[4,32,32,128]{3,2,1,0:T(8,128)S(1)}, f32[4,32,32,128]{3,2,1,0:T(8,128)}, u32[]{:S(2)}) copy-start(f32[4,32,32,128]{3,2,1,0:T(8,128)} %param.13) | copy-start | bytes 6291460
  501.3 11.6 %collective-permute-start.4 = (f32[2,24,24,128]{3,2,1,0:T(8,128)S(1)}, f32[2,24,24,128]{3,2,1,0:T(8,128)S(1)}, u32[]{:S(2)}, u32[]{:S(2)}) collective-permute-start(f32[2,24,24,128]{3,2,1,0:T(8,128)S(1)} %pad_maximum_fusion.7), channel_id=1, source_target_pairs={{0,7},{1,0},{2,1},{3,2},{4,3},{5,4},{6,5},{7,6},{8,15},{9,8},{10,9... | collective-permute-start | bytes 1769480 | tf_op jit(solution)/shard_map/ppermute | solution.py:24
  514.4 49.7 %collective-permute-start.5 = (f32[2,24,88,128]{3,2,1,0:T(8,128)}, f32[2,24,88,128]{3,2,1,0:T(8,128)}, u32[]{:S(2)}, u32[]{:S(2)}) collective-permute-start(f32[2,24,88,128]{3,2,1,0:T(8,128)} %pad_maximum_fusion.1), channel_id=1, source_target_pairs={{0,248},{8,0},{16,8},{24,16},{32,24},{40,32},{48,40},{56,48},{64,5... | collective-permute-start | bytes 6488072 | tf_op jit(solution)/shard_map/ppermute | solution.py:24
  520.7 43.3 %copy-start.3 = (f32[128,64,24]{0,1,2:T(8,128)S(1)}, f32[128,64,24]{0,1,2:T(8,128)}, u32[]{:S(2)}) copy-start(f32[128,64,24]{0,1,2:T(8,128)} %copy-done.2) | copy-start | bytes 2359300
where the time goes:
time: 580 us; the launch traced here: 571 us
  matrix products  171 us (29%)
  waiting for transfers between devices  140 us (24%)
  blocking collectives  115 us (20%)
  local copies, waits for them, and re-layouts  69 us (12%)
  other arithmetic  35.5 us (6%)
  starting transfers between devices  20 us (3%)
  between operations  19.6 us (3%)
    dot_general x20, matrix products, product(): return jnp.einsum(pattern, operand, table_mat, precision=precise_mode)  171 us
    ppermute x6, waiting for transfers between devices, from_behind(): lax.ppermute(shard, axis, [(i, (i + by) % peers) for i in range(peers)])  104 us
    all_to_all x2, blocking collectives, cut_exchange(): lax.all_to_all(section, axis, split_axis=0, concat_axis=0, tiled=True)  43.4 us
    all_to_all x1, blocking collectives, on_device(): lax.all_to_all(jnp.stack([depth_real, depth_imag]), 'px', split_axis=1, c...  40.9 us
    all_to_all x1, waiting for transfers between devices, on_device(): lax.all_to_all(jnp.stack([rows_real, rows_imag]), 'px', split_axis=3, con...  35.9 us
    all_to_all x1, blocking collectives, on_device(): lax.all_to_all(jnp.stack([back_real, back_imag]), 'py', split_axis=2, con...  31.1 us
    dynamic_update_slice x4, local copies, waits for them, and re-layouts, on_device(): box_patch = lax.dynamic_update_slice(box_patch, current + contrib, position)  24.2 us
    unnamed x25, local copies, waits for them, and re-layouts  17.4 us
  transfers between devices with their start and end apart: 7, of which 5 were waited for; matrix products, arithmetic and copies ran while one was open for 1% of the time, Pallas kernels for 0%

commit v1 on v0

v1 whole, which is shorter than its diff:
```python
import functools

import jax
import jax.numpy as jnp
import numpy as np
from jax import lax
from jax.experimental import pallas as pl
from jax.experimental.pallas import tpu as pltpu
from jax.sharding import PartitionSpec as P

NX, NY, NZ = 768, 512, 128
STEP = 8
PX, PY = 32, 8
CX, CY = NX // PX, NY // PY
OV = 24
KX = NX // PY
F32 = jnp.float32
BF16 = jnp.bfloat16
SPECIAL = 16
RATE = 0.2
GRADIENT = 0.1
COUPLING = 1.5

VM = pl.BlockSpec(memory_space=pltpu.VMEM)
SM = pl.BlockSpec(memory_space=pltpu.SMEM)


def halves(array):
    high = np.asarray(array, np.float32).astype(jnp.bfloat16)
    low = (np.asarray(array, np.float64) - high.astype(np.float64)).astype(jnp.bfloat16)
    return high, low


def slot_wave(p, h):
    if h == 0:
        return 4 * p + 1
    return 4 * p + 2 if p < 16 else 4 * p


def depth_tables():
    z = np.arange(NZ)
    forward = np.zeros((NZ, NZ))
    inverse = np.zeros((NZ, NZ))
    total = NX * NY * NZ
    for h in range(2):
        for p in range(PX):
            row_re, row_im = h * 64 + p, h * 64 + 32 + p
            wave = slot_wave(p, h)
            cosine = np.cos(2 * np.pi * ((wave * z) % NZ) / NZ)
            sine = np.sin(2 * np.pi * ((wave * z) % NZ) / NZ)
            if p == SPECIAL and h == 1:
                forward[row_re], forward[row_im] = 1.0, (-1.0) ** z
                inverse[row_re], inverse[row_im] = 1.0 / total, (-1.0) ** z / total
            else:
                forward[row_re], forward[row_im] = cosine, -sine
                inverse[row_re], inverse[row_im] = 2 * cosine / total, -2 * sine / total
    return forward, inverse


def wave_rows(count, step, length):
    angle = 2 * np.pi * ((step * np.arange(count)[:, None] * np.arange(length)[None]) % length) / length
    return np.stack([np.cos(angle), np.sin(angle)]).astype(np.float32)


def column_tables():
    k = np.arange(NY)
    angle = 2 * np.pi * ((k[:, None] * k[None]) % NY) / NY
    return halves(np.concatenate([np.cos(angle), np.sin(angle)], axis=1))


def mirror_tables():
    rows = np.zeros((KX, KX), np.float32)
    for j in range(1, KX):
        rows[j, KX - j] = 1.0
    lanes = np.zeros((NY, NY), np.float32)
    for k in range(NY):
        lanes[(NY - k) % NY, k] = 1.0
    return rows.astype(jnp.bfloat16), lanes.astype(jnp.bfloat16)


def split(value):
    high = value.astype(BF16)
    return high, (value - high.astype(F32)).astype(BF16)


def dot(a, b):
    return jnp.dot(a, b, preferred_element_type=F32)


def dot3(a, b):
    return dot(a[0], b[0]) + dot(a[0], b[1]) + dot(a[1], b[0])


def turn(value):
    return pltpu.roll(value, 64, axis=value.ndim - 1)


def low_lanes(shape):
    return lax.broadcasted_iota(jnp.int32, shape, len(shape) - 1) < 64


def call(kernel, outs, specs, args, scratch=(), **params):
    return pl.pallas_call(
        kernel,
        out_shape=outs,
        in_specs=specs,
        out_specs=jax.tree.map(lambda unused: VM, outs),
        scratch_shapes=scratch,
        compiler_params=pltpu.CompilerParams(vmem_limit_bytes=60 * 1024 * 1024, **params),
    )(*args)


def shaped(*shape, dtype=F32):
    return jax.ShapeDtypeStruct(shape, dtype)


def place_kernel(start, ids, misfit, eta, own_e, next_e, side_e, corner_e, own_o, next_o, side_o, corner_o, field, cover):
    field[...] = jnp.zeros_like(field)
    cover[...] = jnp.zeros_like(cover)
    for b in range(eta.shape[0]):
        weight = misfit[ids[b]]
        sx = start[0, b]
        sy = pl.multiple_of(start[1, b], 8)

        def body(i, unused):
            value = eta[b, i]
            square = value * value
            rows = pl.ds(sy, 32)
            field[sx + i, rows, :] = field[sx + i, rows, :] + weight * square
            cover[sx + i, rows, :] = cover[sx + i, rows, :] + square
            return unused

        lax.fori_loop(0, 32, body, 0, unroll=4)
    for source, own, beside, side, corner in ((field, own_e, next_e, side_e, corner_e), (cover, own_o, next_o, side_o, corner_o)):
        own[...] = source[:CX, :CY]
        beside[...] = source[CX:, :CY]
        side[...] = source[:CX, CY:]
        corner[...] = source[CX:, CY:]


def gather_kernel(own, beside, side, corner, out, first):
    out[...] = own[...] + beside[...]
    out[:, :OV] = out[:, :OV] + (side[...] + corner[...])
    first[...] = out[:, :OV]


def depth_kernel(own, beside, side, corner, wave_h, wave_l, out, field):
    field[...] = own[...] + beside[...]
    field[:, :OV] = field[:, :OV] + (side[...] + corner[...])
    waves = (wave_h[...], wave_l[...])
    keep = low_lanes((PX, 128))
    nt = (((1,), (1,)), ((), ()))
    for group in range(CX // 4):
        rows = split(field[4 * group : 4 * group + 4].reshape(256, NZ))
        spectrum = (
            lax.dot_general(waves[0], rows[0], nt, preferred_element_type=F32)
            + lax.dot_general(waves[0], rows[1], nt, preferred_element_type=F32)
            + lax.dot_general(waves[1], rows[0], nt, preferred_element_type=F32)
        )
        for tile in range(2):
            for h in range(2):
                real = spectrum[64 * h : 64 * h + 32, 128 * tile : 128 * tile + 128]
                imag = spectrum[64 * h + 32 : 64 * h + 64, 128 * tile : 128 * tile + 128]
                x = 4 * group + 2 * tile
                out[pl.ds(24 * h + x, PX, stride=48), :] = jnp.where(keep, real, turn(imag))
                out[pl.ds(24 * h + x + 1, PX, stride=48), :] = jnp.where(keep, turn(real), imag)


def undepth_kernel(spectra, wave_h, wave_l, out, first):
    waves = (wave_h[...], wave_l[...])
    keep = low_lanes((PX, 128))
    for tile in range(CX // 2):
        x = 2 * tile
        parts = []
        for h in range(2):
            even = spectra[pl.ds(24 * h + x, PX, stride=48), :]
            odd = spectra[pl.ds(24 * h + x + 1, PX, stride=48), :]
            parts.append(jnp.where(keep, even, turn(odd)))
            parts.append(jnp.where(keep, turn(even), odd))
        block = split(jnp.concatenate(parts, axis=0).T)
        out[x : x + 2] = dot3(block, waves).reshape(2, CY, NZ)
    first[...] = out[:, :OV]


def table_kernel(coarse, fine, cos_h, cos_l, sin_h, sin_l):
    fine_c, fine_s = fine[0], fine[1]

    def body(k, unused):
        coarse_c, coarse_s = coarse[0, pl.ds(k, 1), :], coarse[1, pl.ds(k, 1), :]
        rows = pl.ds(pl.multiple_of(32 * k, 32), 32)
        cos_h[rows, :], cos_l[rows, :] = split(coarse_c * fine_c - coarse_s * fine_s)
        sin_h[rows, :], sin_l[rows, :] = split(coarse_s * fine_c + coarse_c * fine_s)
        return unused

    lax.fori_loop(0, NX // 32, body, 0)


def rows_kernel(place, lines, cos_h, cos_l, sin_h, sin_l, out):
    data = split(jnp.concatenate([lines[:, 0].reshape(NX, 128), lines[:, 1].reshape(NX, 128)], axis=1))
    keep = low_lanes((KX, 128))
    special = place[0] == SPECIAL
    for q in range(PY):
        rows = slice(KX * q, KX * q + KX)
        cosine = dot3((cos_h[rows], cos_l[rows]), data)
        sine = dot3((sin_h[rows], sin_l[rows]), data)
        for h in range(2):
            real, imag = cosine[:, 128 * h : 128 * h + 128], sine[:, 128 * h : 128 * h + 128]
            turned = turn(imag)
            normal = jnp.where(keep, real + turned, real - turned)
            if h == 1:
                if q < 4:
                    parted = jnp.where(keep, real, -turned)
                else:
                    parted = jnp.where(keep, turn(real), -imag)
                if q % 4 == 0:
                    parted = jnp.where(lax.broadcasted_iota(jnp.int32, (KX, 128), 0) == 0, real, parted)
                normal = jnp.where(special, parted, normal)
            out[q, h] = normal


def unrows_kernel(place, lines, cos_h, cos_l, sin_h, sin_l, out, one_h, one_l, two_h, two_l):
    keep = low_lanes((KX, 128))
    special = place[0] == SPECIAL
    for q in range(PY):
        rows = slice(KX * q, KX * q + KX)
        for h in range(2):
            value = lines[q, h]
            turned = turn(value)
            first = value
            second = jnp.where(keep, -turned, turned)
            if h == 1:
                if q < 4:
                    parted_1 = jnp.where(keep, 2.0 * value, 0.0)
                    parted_2 = jnp.where(keep, -2.0 * turned, 0.0)
                else:
                    parted_1 = jnp.where(keep, 0.0, 2.0 * turned)
                    parted_2 = jnp.where(keep, 0.0, -2.0 * value)
                if q % 4 == 0:
                    top = lax.broadcasted_iota(jnp.int32, (KX, 128), 0) == 0
                    parted_1 = jnp.where(top, value, parted_1)
                    parted_2 = jnp.where(top, 0.0, parted_2)
                first = jnp.where(special, parted_1, first)
                second = jnp.where(special, parted_2, second)
            lanes = slice(128 * h, 128 * h + 128)
            one_h[rows, lanes], one_l[rows, lanes] = split(first)
            two_h[rows, lanes], two_l[rows, lanes] = split(second)
    one = (one_h[...], one_l[...])
    two = (two_h[...], two_l[...])
    for block in range(8):
        rows = slice(96 * block, 96 * block + 96)
        result = dot3((cos_h[rows], cos_l[rows]), one) + dot3((sin_h[rows], sin_l[rows]), two)
        for h in range(2):
            out[4 * block : 4 * block + 4, h] = result[:, 128 * h : 128 * h + 128].reshape(4, CX, 128)


def green_kernel(place, own, near, far, extra, near_row, far_row, extra_row, row_flip, lane_flip, out, out_extra):
    p, q = place[0], place[1]
    special = p == SPECIAL
    upper = special & (q >= 4)
    lower = special & (q < 4)
    flips = row_flip[...]
    lanes = lane_flip[...]

    def permute(value):
        high, low = split(value)
        return dot(high, lanes) + dot(low, lanes)

    def mirror(plane, row):
        high, low = split(plane)
        turned = dot(flips, high) + dot(flips, low)
        top = lax.broadcasted_iota(jnp.int32, turned.shape, 0) == 0
        return permute(jnp.where(top, jnp.broadcast_to(row, turned.shape), turned))

    out[0] = 0.5 * (own[1] + mirror(near[...], near_row[0:1]))
    base = jnp.where(p < 16, own[2], jnp.where(lower, extra[...], own[0]))
    plane = jnp.where(upper, extra[...], far[...])
    row = jnp.where(upper, extra_row[0:1], far_row[0:1])
    second = 0.5 * (base + mirror(plane, row))
    packed = jnp.concatenate([jnp.broadcast_to(far_row[0:1], (8, NY)), jnp.broadcast_to(own[0, 0:1], (8, NY))], axis=0)
    packed = 0.5 * (packed + permute(packed))
    top = (lax.broadcasted_iota(jnp.int32, (KX, NY), 0) == 0) & special & (q % 4 == 0)
    out[1] = jnp.where(top, jnp.broadcast_to(packed[0:1], (KX, NY)), second)
    out_extra[...] = packed[8:16]


def columns_kernel(place, lines, green, green_extra, table_h, table_l, out, work_h, work_l):
    keep = low_lanes((KX, 128))
    packed = (place[0] == SPECIAL) & (place[1] % 4 == 0)
    for h in range(2):
        for tile in range(4):
            even, odd = lines[2 * tile, h], lines[2 * tile + 1, h]
            lanes = slice(128 * tile, 128 * tile + 128)
            rows = slice(192 * h, 192 * h + 96)
            work_h[rows, lanes], work_l[rows, lanes] = split(jnp.where(keep, even, turn(odd)))
            rows = slice(192 * h + 96, 192 * h + 192)
            work_h[rows, lanes], work_l[rows, lanes] = split(jnp.where(keep, turn(even), odd))
    tables = (table_h[...], table_l[...])
    wave = dot3((work_h[0:384], work_l[0:384]), tables)
    top = (lax.broadcasted_iota(jnp.int32, (KX, NY), 0) == 0) & packed
    for h in range(2):
        re_c, re_s = wave[192 * h : 192 * h + 96, :NY], wave[192 * h : 192 * h + 96, NY:]
        im_c, im_s = wave[192 * h + 96 : 192 * h + 192, :NY], wave[192 * h + 96 : 192 * h + 192, NY:]
        real, imag = re_c + im_s, im_c - re_s
        if h == 1:
            real, imag = jnp.where(top, re_c, real), jnp.where(top, -re_s, imag)
            fix = green_extra[...]
            work_h[384:392], work_l[384:392] = split(fix * im_c[0:8])
            work_h[392:400], work_l[392:400] = split(fix * -im_s[0:8])
        work_h[192 * h : 192 * h + 96], work_l[192 * h : 192 * h + 96] = split(green[h] * real)
        work_h[192 * h + 96 : 192 * h + 192], work_l[192 * h + 96 : 192 * h + 192] = split(green[h] * imag)
    wave = dot3((work_h[...], work_l[...]), tables)
    for h in range(2):
        real = wave[192 * h : 192 * h + 96, :NY] - wave[192 * h + 96 : 192 * h + 192, NY:]
        imag = wave[192 * h + 96 : 192 * h + 192, :NY] + wave[192 * h : 192 * h + 96, NY:]
        if h == 1:
            fix = wave[384:392, :NY] - wave[392:400, NY:]
            imag = jnp.where(top, jnp.broadcast_to(fix[0:1], (KX, NY)), imag)
        for tile in range(4):
            lanes = slice(128 * tile, 128 * tile + 128)
            re, im = real[:, lanes], imag[:, lanes]
            out[2 * tile, h] = jnp.where(keep, re, turn(im))
            out[2 * tile + 1, h] = jnp.where(keep, turn(re), im)


def update_kernel(start, ids, misfit, eta, mu_own, mu_side, mu_next, mu_corner, oc_own, oc_side, oc_next, oc_corner, out, field, cover):
    for source, own, side, beside, corner in (
        (field, mu_own, mu_side, mu_next, mu_corner),
        (cover, oc_own, oc_side, oc_next, oc_corner),
    ):
        source[:CX, :CY] = own[...]
        source[:CX, CY:] = side[...]
        source[CX:, :CY] = beside[...]
        source[CX:, CY:] = corner[...]
    sublane = lax.broadcasted_iota(jnp.int32, (32, NZ), 0)
    for b in range(eta.shape[0]):
        weight = misfit[ids[b]]
        sx = start[0, b]
        sy = pl.multiple_of(start[1, b], 8)

        def body(i, unused):
            value = eta[b, i]
            before = jnp.where(i > 0, eta[b, jnp.maximum(i - 1, 0)], 0.0)
            after = jnp.where(i < 31, eta[b, jnp.minimum(i + 1, 31)], 0.0)
            above = jnp.where(sublane == 0, 0.0, pltpu.roll(value, 1, axis=0))
            below = jnp.where(sublane == 31, 0.0, pltpu.roll(value, 31, axis=0))
            lap = before + after + above + below + pltpu.roll(value, 1, axis=1) + pltpu.roll(value, 127, axis=1) - 6.0 * value
            mu = field[sx + i, pl.ds(sy, 32), :]
            total = cover[sx + i, pl.ds(sy, 32), :]
            square = value * value
            force = value * square - value + 2.0 * COUPLING * value * (total - square)
            force = force - GRADIENT * lap + 2.0 * weight * value * mu
            out[b, i] = value - RATE * force
            return unused

        lax.fori_loop(0, 32, body, 0, unroll=2)


def shift(value, axis, by):
    peers = lax.axis_size(axis)
    return lax.ppermute(value, axis, [(i, (i + by) % peers) for i in range(peers)])


def both(value, pairs):
    return lax.ppermute(value, ("px", "py"), [(a * PY + b, c * PY + d) for (a, b), (c, d) in pairs])


def exchange(value, axis):
    return lax.all_to_all(value, axis, split_axis=0, concat_axis=0, tiled=True)


def green_parts(green, p):
    devices = [(a, b) for a in range(PX) for b in range(PY)]

    def far_of(a):
        return 31 - a if a >= 16 else (32 - a if a else SPECIAL)

    far_plane = jnp.where(p < 16, green[0], green[2])
    near = both(green[3], [((a, b), (31 - a, 7 - b)) for a, b in devices])
    far = both(far_plane, [((a, b), (far_of(a), 7 - b)) for a, b in devices])
    extra = both(
        green[0],
        [((0, b), (SPECIAL, b)) for b in range(4)] + [((SPECIAL, 7 - b), (SPECIAL, b)) for b in range(4, 8)],
    )
    near_row = both(green[3, :8], [((a, b), (31 - a, (8 - b) % 8)) for a, b in devices])
    far_row = both(far_plane[:8], [((a, b), (far_of(a), (8 - b) % 8)) for a, b in devices])
    extra_row = both(green[0, :8], [((SPECIAL, 8 - b), (SPECIAL, b)) for b in range(5, 8)])
    return near, far, extra, near_row, far_row, extra_row


def on_device(eta, corners, grain_ids, misfit, green):
    p, q = lax.axis_index("px"), lax.axis_index("py")
    place = jnp.stack([p, q]).astype(jnp.int32)
    start = jnp.stack([corners[:, 0] * STEP - p * CX, corners[:, 1] * STEP - q * CY]).astype(jnp.int32)
    forward, inverse = depth_tables()
    coarse, fine = wave_rows(24, 32, NX), wave_rows(32, 1, NX)
    columns = column_tables()

    near, far, extra, near_row, far_row, extra_row = green_parts(green, p)
    piece = [shaped(CX, CY, NZ), shaped(CX, CY, NZ), shaped(CX, OV, NZ), shaped(CX, OV, NZ)]
    patch = (CX + OV, CY + OV, NZ)
    own_e, next_e, side_e, corner_e, own_o, next_o, side_o, corner_o = call(
        place_kernel, piece + piece, [SM, SM, SM, VM], (start, grain_ids, misfit, eta), scratch=[pltpu.VMEM(patch, F32)] * 2
    )
    tables = call(table_kernel, [shaped(NX, NX, dtype=BF16)] * 4, [VM] * 2, (coarse, fine))

    def summed(beside, side, corner):
        return shift(beside, "px", 1), shift(side, "py", 1), shift(shift(corner, "py", 1), "px", 1)

    got_e = summed(next_e, side_e, corner_e)
    lines = call(
        depth_kernel, shaped(PX * 48, 128), [VM] * 6, (own_e, *got_e, *halves(forward)), scratch=[pltpu.VMEM((CX, CY, NZ), F32)]
    )
    lines = exchange(lines.reshape(PX, 2, CX, 128), "px")
    lines = call(rows_kernel, shaped(PY, 2, KX, 128), [SM] + [VM] * 5, (place, lines, *tables))
    lines = exchange(lines, "py")
    symmetric, symmetric_extra = call(
        green_kernel,
        [shaped(2, KX, NY), shaped(8, NY)],
        [SM] + [VM] * 9,
        (place, green, near, far, extra, near_row, far_row, extra_row, *mirror_tables()),
    )
    lines = call(
        columns_kernel,
        shaped(PY, 2, KX, 128),
        [SM] + [VM] * 5,
        (place, lines, symmetric, symmetric_extra, *columns),
        scratch=[pltpu.VMEM((400, NY), BF16)] * 2,
    )
    lines = exchange(lines, "py")
    lines = call(
        unrows_kernel,
        shaped(PX, 2, CX, 128),
        [SM] + [VM] * 5,
        (place, lines, *tables),
        scratch=[pltpu.VMEM((NX, 256), BF16)] * 4,
    )
    lines = exchange(lines, "px")
    potential, first = call(
        undepth_kernel,
        [shaped(CX, CY, NZ), shaped(CX, OV, NZ)],
        [VM] * 3,
        (lines.reshape(PX * 48, 128), *halves(inverse)),
    )

    def window(own, begin):
        side = shift(begin, "py", -1)
        return own, side, shift(own, "px", -1), shift(side, "px", -1)

    got_o = summed(next_o, side_o, corner_o)
    occupancy, first_o = call(gather_kernel, [shaped(CX, CY, NZ), shaped(CX, OV, NZ)], [VM] * 4, (own_o, *got_o))
    eta_next = call(
        update_kernel,
        shaped(*eta.shape),
        [SM] * 3 + [VM] * 9,
        (start, grain_ids, misfit, eta, *window(potential, first), *window(occupancy, first_o)),
        scratch=[pltpu.VMEM(patch, F32)] * 2,
    )
    return eta_next, potential


def solution(mesh):
    in_specs = (P(("px", "py"), None, None, None), P(("px", "py"), None), P(("px", "py")), P(), P("px", "py", None))
    out_specs = (P(("px", "py"), None, None, None), P("px", "py", None))
    return jax.shard_map(on_device, mesh=mesh, in_specs=in_specs, out_specs=out_specs, check_vma=False)
```

time: 580 us -> 260 us (0.45); the launches traced: 571 us -> 259 us
  matrix products: 171 us -> 0 us
  blocking collectives: 115 us -> 17.8 us
  local copies, waits for them, and re-layouts: 69 us -> 7.55 us
  Pallas kernels: 0 us -> 50.5 us
  other arithmetic: 35.5 us -> 1.9 us
  starting transfers between devices: 20 us -> 53 us
  between operations: 19.6 us -> 0.81 us
  waiting for transfers between devices: 140 us -> 128 us
    dot_general x20 -> x0, matrix products: 171 us -> none  [product(): return jnp.einsum(pattern, operand, table_mat, precision=precise_mode)]
    all_to_all x4 -> x1, blocking collectives: 115 us -> 17.8 us  [exchange(): return lax.all_to_all(value, axis, split_axis=0, concat_axis=0, tiled=True)]
    pallas_call x0 -> x10, Pallas kernels: none -> 50.5 us  [call(): pl.pallas_call(kernel, out_shape=outs, in_specs=specs, out_specs=jax.tree...]
    dynamic_update_slice x4 -> x0, local copies, waits for them, and re-layouts: 24.2 us -> none  [on_device(): box_patch = lax.dynamic_update_slice(box_patch, current + contrib, position)]
    all_to_all x1 -> x3, waiting for transfers between devices: 35.9 us -> 13.8 us  [exchange(): return lax.all_to_all(value, axis, split_axis=0, concat_axis=0, tiled=True)]
    ppermute x6 -> x20, starting transfers between devices: 14.5 us -> 32.7 us  [the longest x14 17.6 us: shift(): lax.ppermute(value, axis, [(i, (i + by) % peers) for i in range(peers)])]
    all_to_all x1 -> x3, starting transfers between devices: 5.52 us -> 20.3 us  [exchange(): return lax.all_to_all(value, axis, split_axis=0, concat_axis=0, tiled=True)]
    all_to_all x2 -> x0, other arithmetic: 11.8 us -> none  [the longest x1 5.91 us: on_device(): lax.all_to_all(jnp.stack([rows_real, rows_imag]), 'px', split_axis=3, con...]
  transfers between devices with their start and end apart: 7 -> 23, of which waited for: 5 -> 14; matrix products, arithmetic and copies ran while one was open for 1% -> 0% of each run, Pallas kernels for 0% -> 5%
where the time goes in v1:
time: 260 us; the launch traced here: 259 us
  waiting for transfers between devices  128 us (49%)
  starting transfers between devices  53 us (20%)
  Pallas kernels  50.5 us (19%)
  blocking collectives  17.8 us (7%)
  local copies, waits for them, and re-layouts  7.55 us (3%)
    ppermute x14, waiting for transfers between devices, shift(): lax.ppermute(value, axis, [(i, (i + by) % peers) for i in range(peers)])  103 us
    pallas_call x10, Pallas kernels, call(): pl.pallas_call(kernel, out_shape=outs, in_specs=specs, out_specs=jax.tree...  50.5 us
    all_to_all x3, starting transfers between devices, exchange(): return lax.all_to_all(value, axis, split_axis=0, concat_axis=0, tiled=True)  20.3 us
    all_to_all x1, blocking collectives, exchange(): return lax.all_to_all(value, axis, split_axis=0, concat_axis=0, tiled=True)  17.8 us
    ppermute x14, starting transfers between devices, shift(): lax.ppermute(value, axis, [(i, (i + by) % peers) for i in range(peers)])  17.6 us
    ppermute x6, starting transfers between devices, both(): lax.ppermute(value, ('px', 'py'), [(a * PY + b, c * PY + d) for (a, b), (...  15.1 us
    all_to_all x3, waiting for transfers between devices, exchange(): return lax.all_to_all(value, axis, split_axis=0, concat_axis=0, tiled=True)  13.8 us
    ppermute x6, waiting for transfers between devices, both(): lax.ppermute(value, ('px', 'py'), [(a * PY + b, c * PY + d) for (a, b), (...  10.7 us
  transfers between devices with their start and end apart: 23, of which 14 were waited for; matrix products, arithmetic and copies ran while one was open for 0% of the time, Pallas kernels for 5%

profile of v1, /device:TPU:1, one launch (start us, length us, event | category | flops | bytes accessed | tf_op | source)
XLA Modules:
  0.0 259.5 jit_solution(15062423040719825616)
XLA Ops:
  1.9 4.5 %shard_map.158 = (f32[24,64,128]{2,1,0:T(8,128)}, f32[24,64,128]{2,1,0:T(8,128)}, f32[24,24,128]{2,1,0:T(8,128)}, f32[24,24,128]{2,1,0:T(8,128)}, f32[24,64,128]...) custom-call(s32[2,4]{1,0:T(2,128)} %pad_add_fusion.start, s32[4]{0:T(128)} %ids.3, ...), custom_call_target="tpu_custom_call" | custom-call | tf_op jit(solution)/shard_map/pallas_call | solution.py:103
  11.0 4.0 %collective-permute-done.2 = f32[24,24,128]{2,1,0:T(8,128)S(1)} collective-permute-done((f32[24,24,128]{2,1,0:T(8,128)}, f32[24,24,128]{2,1,0:T(8,128)S(1)}, u32[]{:S(2)}, u32[]{:S(2)}) %collective-permute-start.2) | collective-permute-done | bytes 294944 | tf_op jit(solution)/shard_map/ppermute | solution.py:360
  18.1 21.1 %collective-permute-done.3.corner = f32[24,24,128]{2,1,0:T(8,128)S(1)} collective-permute-done((f32[24,24,128]{2,1,0:T(8,128)S(1)}, f32[24,24,128]{2,1,0:T(8,128)S(1)}, u32[]{:S(2)}, u32[]{:S(2)}) %collective-permute-start.3) | collective-permute-done | bytes 294944 | tf_op jit(solution)/shard_map/ppermute | solution.py:360
  40.1 3.0 %shard_map.159 = f32[1536,128]{1,0:T(8,128)} custom-call(f32[24,64,128]{2,1,0:T(8,128)} %get-tuple-element.20.own, f32[24,64,128]{2,1,0:T(8,128)} %copy-done.7, f32[24,24,128]{2,1,0:T(8,128)} %copy-done.11, f32[24,24,128]{2,1,0:T(8,128)} %copy-done.13, bf16[128,128]{1,0:T(8,128)(2,1)} %constant.39.clone.wave_h, bf16[128,128]{1,0:T(8,128)(2,1)} %constant.40.clone.wave_l), custom_call_target="tpu_custom_call" | custom-call | tf_op jit(solution)/shard_map/pallas_call | solution.py:103
  43.2 5.5 %all-to-all-start = ((f32[32,2,24,128]{3,2,1,0:T(8,128)}), f32[32,2,24,128]{3,2,1,0:T(8,128)S(1)}, u32[]{:S(2)}, u32[]{:S(2)}) async-start(f32[32,2,24,128]{3,2,1,0:T(8,128)} %bitcast.21), calls=%async_computation | async-start | bytes 1572864 | tf_op jit(solution)/shard_map/all_to_all | solution.py:368
  48.7 4.4 %shard_map.160 = (bf16[768,768]{1,0:T(8,128)(2,1)}, bf16[768,768]{1,0:T(8,128)(2,1)}, bf16[768,768]{1,0:T(8,128)(2,1)}, bf16[768,768]{1,0:T(8,128)(2,1)}) custom-call(f32[2,24,768]{2,1,0:T(8,128)} %constant.37.clone.coarse, f32[2,32,768]{2,1,0:T(8,128)} %constant.38.clone.fine), custom_call_target="tpu_custom_call" | custom-call | tf_op jit(solution)/shard_map/pallas_call | solution.py:103
  53.6 13.8 %all-to-all-done.lines = f32[32,2,24,128]{3,2,1,0:T(8,128)S(1)} async-done(((f32[32,2,24,128]{3,2,1,0:T(8,128)}), f32[32,2,24,128]{3,2,1,0:T(8,128)S(1)}, u32[]{:S(2)}, u32[]{:S(2)}) %all-to-all-start) | async-done | bytes 786464 | tf_op jit(solution)/shard_map/all_to_all | solution.py:368
  68.3 6.7 %shard_map.161 = f32[8,2,96,128]{3,2,1,0:T(8,128)} custom-call(s32[2]{0:T(128)} %pad_add_fusion.1.place, f32[32,2,24,128]{3,2,1,0:T(8,128)} %copy-done.2, bf16[768,768]{1,0:T(8,128)(2,1)} %get-tuple-element.24.cos_h, bf16[768,768]{1,0:T(8,128)(2,1)} %get-tuple-element.25.cos_l, bf16[768,768]{1,0:T(8,128)(2,1)} %get-tuple-element.26.sin_h, ...), custom_call_target="tpu_custom_call" | custom-call | tf_op jit(solution)/shard_map/pallas_call | solution.py:103
  75.0 9.9 %all-to-all-start.1 = ((f32[8,2,96,128]{3,2,1,0:T(8,128)}), f32[8,2,96,128]{3,2,1,0:T(8,128)S(1)}, u32[]{:S(2)}, u32[]{:S(2)}) async-start(f32[8,2,96,128]{3,2,1,0:T(8,128)} %shard_map.161), calls=%async_computation.1 | async-start | bytes 1572864 | tf_op jit(solution)/shard_map/all_to_all | solution.py:368
  85.0 3.1 %collective-permute-start.5 = (f32[96,512]{1,0:T(8,128)S(1)}, f32[96,512]{1,0:T(8,128)S(1)}, u32[]{:S(2)}, u32[]{:S(2)}) collective-permute-start(f32[96,512]{1,0:T(8,128)S(1)} %bitcast_select_fusion), channel_id=1, source_target_pairs={{0,135},{1,134},{2,133},{3,132},{4,131},{5,130},{6,129},{7,128},{8... | collective-permute-start | bytes 589832 | tf_op jit(solution)/shard_map/ppermute | solution.py:364
  89.3 5.8 %collective-permute-start.4 = (f32[96,512]{1,0:T(8,128)S(1)}, f32[96,512]{1,0:T(8,128)S(1)}, u32[]{:S(2)}, u32[]{:S(2)}) collective-permute-start(f32[96,512]{1,0:T(8,128)S(1)} %get-tuple-element.41), channel_id=1, source_target_pairs={{0,255},{1,254},{2,253},{3,252},{4,251},{5,250},{6,249},{7,248},{8... | collective-permute-start | bytes 589832 | tf_op jit(solution)/shard_map/ppermute | solution.py:364
  95.1 4.3 %collective-permute-start.6 = (f32[96,512]{1,0:T(8,128)S(1)}, f32[96,512]{1,0:T(8,128)S(1)}, u32[]{:S(2)}, u32[]{:S(2)}) collective-permute-start(f32[96,512]{1,0:T(8,128)S(1)} %get-tuple-element.40), channel_id=1, source_target_pairs={{0,128},{1,129},{2,130},{3,131},{131,132},{130,133},{129,134},{128... | collective-permute-start | bytes 589832 | tf_op jit(solution)/shard_map/ppermute | solution.py:364
  101.9 8.5 %collective-permute-done.7.near_row = f32[8,512]{1,0:T(8,128)S(1)} collective-permute-done((f32[8,512]{1,0:T(8,128)S(1)}, f32[8,512]{1,0:T(8,128)S(1)}, u32[]{:S(2)}, u32[]{:S(2)}) %collective-permute-start.7) | collective-permute-done | bytes 16416 | tf_op jit(solution)/shard_map/ppermute | solution.py:364
  112.2 3.3 %shard_map.162 = (f32[2,96,512]{2,1,0:T(8,128)}, f32[8,512]{1,0:T(8,128)}) custom-call(s32[2]{0:T(128)} %pad_add_fusion.1.place, f32[4,96,512]{2,1,0:T(8,128)} %own.1, f32[96,512]{1,0:T(8,128)} %copy-done.17, f32[96,512]{1,0:T(8,128)} %copy-done.16, f32[96,512]{1,0:T(8,128)} %copy-done.18, f32[8,512]{1,0:T(8,128)} %copy-done.20, f32[8,512]{1,0:T(8,128)} %copy-done.19, ...), custom_call_target="tpu_custom_call" | custom-call | tf_op jit(solution)/shard_map/pallas_call | solution.py:103
  116.4 5.9 %shard_map.163 = f32[8,2,96,128]{3,2,1,0:T(8,128)} custom-call(s32[2]{0:T(128)} %pad_add_fusion.1.place, f32[8,2,96,128]{3,2,1,0:T(8,128)} %copy-done.1, f32[2,96,512]{2,1,0:T(8,128)} %get-tuple-element.28.green, f32[8,512]{1,0:T(8,128)} %get-tuple-element.29.green_extra, bf16[512,1024]{1,0:T(8,128)(2,1)} %constant.43.clone.table_h, ...), custom_call_target="tpu_custom_call" | custom-call | tf_op jit(solution)/shard_map/pallas_call | solution.py:103
  122.2 17.8 %all_to_all.20.lines = f32[8,2,96,128]{3,2,1,0:T(8,128)} all-to-all(f32[8,2,96,128]{3,2,1,0:T(8,128)} %shard_map.163), channel_id=1, replica_groups=mesh['px'=32,'py'=8] {'py'}, dimensions={0} | all-to-all | bytes 1572864 | tf_op jit(solution)/shard_map/all_to_all | solution.py:368
  140.1 6.8 %shard_map.164 = f32[32,2,24,128]{3,2,1,0:T(8,128)} custom-call(s32[2]{0:T(128)} %pad_add_fusion.1.place, f32[8,2,96,128]{3,2,1,0:T(8,128)} %all_to_all.20.lines, bf16[768,768]{1,0:T(8,128)(2,1)} %get-tuple-element.24.cos_h, bf16[768,768]{1,0:T(8,128)(2,1)} %get-tuple-element.25.cos_l, bf16[768,768]{1,0:T(8,128)(2,1)} %get-tuple-element.26.sin_h, ...), custom_call_target="tpu_custom_call" | custom-call | tf_op jit(solution)/shard_map/pallas_call | solution.py:103
  146.9 4.9 %all-to-all-start.3 = ((f32[32,2,24,128]{3,2,1,0:T(8,128)}), f32[32,2,24,128]{3,2,1,0:T(8,128)S(1)}, u32[]{:S(2)}, u32[]{:S(2)}) async-start(f32[32,2,24,128]{3,2,1,0:T(8,128)} %shard_map.164), calls=%async_computation.3 | async-start | bytes 1572864 | tf_op jit(solution)/shard_map/all_to_all | solution.py:368
  155.2 3.6 %collective-permute-done.15 = f32[24,24,128]{2,1,0:T(8,128)S(1)} collective-permute-done((f32[24,24,128]{2,1,0:T(8,128)S(1)}, f32[24,24,128]{2,1,0:T(8,128)S(1)}, u32[]{:S(2)}, u32[]{:S(2)}) %collective-permute-start.15) | collective-permute-done | bytes 294944 | tf_op jit(solution)/shard_map/ppermute | solution.py:360
  162.0 34.6 %collective-permute-done.16.corner = f32[24,24,128]{2,1,0:T(8,128)S(1)} collective-permute-done((f32[24,24,128]{2,1,0:T(8,128)S(1)}, f32[24,24,128]{2,1,0:T(8,128)S(1)}, u32[]{:S(2)}, u32[]{:S(2)}) %collective-permute-start.16) | collective-permute-done | bytes 294944 | tf_op jit(solution)/shard_map/ppermute | solution.py:360
  208.6 5.1 %collective-permute-done.17.oc_side = f32[24,24,128]{2,1,0:T(8,128)S(1)} collective-permute-done((f32[24,24,128]{2,1,0:T(8,128)}, f32[24,24,128]{2,1,0:T(8,128)S(1)}, u32[]{:S(2)}, u32[]{:S(2)}) %collective-permute-start.17) | collective-permute-done | bytes 294944 | tf_op jit(solution)/shard_map/ppermute | solution.py:360
  218.0 23.2 %collective-permute-done.19.oc_corner = f32[24,24,128]{2,1,0:T(8,128)S(1)} collective-permute-done((f32[24,24,128]{2,1,0:T(8,128)S(1)}, f32[24,24,128]{2,1,0:T(8,128)S(1)}, u32[]{:S(2)}, u32[]{:S(2)}) %collective-permute-start.19) | collective-permute-done | bytes 294944 | tf_op jit(solution)/shard_map/ppermute | solution.py:360
  241.2 6.3 %collective-permute-done.12.mu_corner = f32[24,24,128]{2,1,0:T(8,128)S(1)} collective-permute-done((f32[24,24,128]{2,1,0:T(8,128)S(1)}, f32[24,24,128]{2,1,0:T(8,128)S(1)}, u32[]{:S(2)}, u32[]{:S(2)}) %collective-permute-start.12) | collective-permute-done | bytes 294944 | tf_op jit(solution)/shard_map/ppermute | solution.py:360
  249.1 10.3 %shard_map.167 = f32[4,32,32,128]{3,2,1,0:T(8,128)} custom-call(s32[2,4]{1,0:T(2,128)} %pad_add_fusion.start, s32[4]{0:T(128)} %ids.3, f32[24]{0:T(128)} %misfit.3, f32[4,32,32,128]{3,2,1,0:T(8,128)} %eta.3, f32[24,64,128]{2,1,0:T(8,128)} %get-tuple-element.19.mu_own, f32[24,24,128]{2,1,0:T(8,128)} %copy-done.9, f32[24,64,128]{2,1,0:T(8,128)} %copy-done.5, ...), custom_call_target="tpu_custom_call" | custom-call | tf_op jit(solution)/shard_map/pallas_call | solution.py:103
  (90 shorter events, 42.3 us)
Async XLA Ops:
  6.4 32.7 %collective-permute-start = (f32[24,64,128]{2,1,0:T(8,128)}, f32[24,64,128]{2,1,0:T(8,128)S(1)}, u32[]{:S(2)}, u32[]{:S(2)}) collective-permute-start(f32[24,64,128]{2,1,0:T(8,128)} %get-tuple-element.21), channel_id=1, source_target_pairs={{0,8},{8,16},{16,24},{24,32},{32,40},{40,48},{48,56},{56,64},{64,7... | collective-permute-start | bytes 2359304 | tf_op jit(solution)/shard_map/ppermute | solution.py:360
  8.9 6.0 %collective-permute-start.2 = (f32[24,24,128]{2,1,0:T(8,128)}, f32[24,24,128]{2,1,0:T(8,128)S(1)}, u32[]{:S(2)}, u32[]{:S(2)}) collective-permute-start(f32[24,24,128]{2,1,0:T(8,128)} %get-tuple-element.23), channel_id=1, source_target_pairs={{0,1},{1,2},{2,3},{3,4},{4,5},{5,6},{6,7},{7,0},{8,9},{9,10},{10,1... | collective-permute-start | bytes 884744 | tf_op jit(solution)/shard_map/ppermute | solution.py:360
  10.9 7.1 %collective-permute-start.1 = (f32[24,24,128]{2,1,0:T(8,128)}, f32[24,24,128]{2,1,0:T(8,128)S(1)}, u32[]{:S(2)}, u32[]{:S(2)}) collective-permute-start(f32[24,24,128]{2,1,0:T(8,128)} %get-tuple-element.22), channel_id=1, source_target_pairs={{0,1},{1,2},{2,3},{3,4},{4,5},{5,6},{6,7},{7,0},{8,9},{9,10},{10,1... | collective-permute-start | bytes 884744 | tf_op jit(solution)/shard_map/ppermute | solution.py:360
  14.9 24.2 %collective-permute-start.3 = (f32[24,24,128]{2,1,0:T(8,128)S(1)}, f32[24,24,128]{2,1,0:T(8,128)S(1)}, u32[]{:S(2)}, u32[]{:S(2)}) collective-permute-start(f32[24,24,128]{2,1,0:T(8,128)S(1)} %collective-permute-done.2), channel_id=1, source_target_pairs={{0,8},{8,16},{16,24},{24,32},{32,40},{40,48},{48,56},{56,64},{64,7... | collective-permute-start | bytes 884744 | tf_op jit(solution)/shard_map/ppermute | solution.py:360
  43.2 24.3 %all-to-all-start = ((f32[32,2,24,128]{3,2,1,0:T(8,128)}), f32[32,2,24,128]{3,2,1,0:T(8,128)S(1)}, u32[]{:S(2)}, u32[]{:S(2)}) async-start(f32[32,2,24,128]{3,2,1,0:T(8,128)} %bitcast.21), calls=%async_computation | async-start | bytes 1572864 | tf_op jit(solution)/shard_map/all_to_all | solution.py:368
  75.0 40.5 %all-to-all-start.1 = ((f32[8,2,96,128]{3,2,1,0:T(8,128)}), f32[8,2,96,128]{3,2,1,0:T(8,128)S(1)}, u32[]{:S(2)}, u32[]{:S(2)}) async-start(f32[8,2,96,128]{3,2,1,0:T(8,128)} %shard_map.161), calls=%async_computation.1 | async-start | bytes 1572864 | tf_op jit(solution)/shard_map/all_to_all | solution.py:368
  85.0 25.4 %collective-permute-start.5 = (f32[96,512]{1,0:T(8,128)S(1)}, f32[96,512]{1,0:T(8,128)S(1)}, u32[]{:S(2)}, u32[]{:S(2)}) collective-permute-start(f32[96,512]{1,0:T(8,128)S(1)} %bitcast_select_fusion), channel_id=1, source_target_pairs={{0,135},{1,134},{2,133},{3,132},{4,131},{5,130},{6,129},{7,128},{8... | collective-permute-start | bytes 589832 | tf_op jit(solution)/shard_map/ppermute | solution.py:364
  88.1 13.1 %collective-permute-start.8 = (f32[8,512]{1,0:T(8,128)S(1)}, f32[8,512]{1,0:T(8,128)S(1)}, u32[]{:S(2)}, u32[]{:S(2)}) collective-permute-start(f32[8,512]{1,0:T(8,128)S(1)} %slice.33), channel_id=1, source_target_pairs={{0,128},{1,135},{2,134},{3,133},{4,132},{5,131},{6,130},{7,129},{8... | collective-permute-start | bytes 49160 | tf_op jit(solution)/shard_map/ppermute | solution.py:364
  89.3 21.6 %collective-permute-start.4 = (f32[96,512]{1,0:T(8,128)S(1)}, f32[96,512]{1,0:T(8,128)S(1)}, u32[]{:S(2)}, u32[]{:S(2)}) collective-permute-start(f32[96,512]{1,0:T(8,128)S(1)} %get-tuple-element.41), channel_id=1, source_target_pairs={{0,255},{1,254},{2,253},{3,252},{4,251},{5,250},{6,249},{7,248},{8... | collective-permute-start | bytes 589832 | tf_op jit(solution)/shard_map/ppermute | solution.py:364
  95.1 15.8 %collective-permute-start.6 = (f32[96,512]{1,0:T(8,128)S(1)}, f32[96,512]{1,0:T(8,128)S(1)}, u32[]{:S(2)}, u32[]{:S(2)}) collective-permute-start(f32[96,512]{1,0:T(8,128)S(1)} %get-tuple-element.40), channel_id=1, source_target_pairs={{0,128},{1,129},{2,130},{3,131},{131,132},{130,133},{129,134},{128... | collective-permute-start | bytes 589832 | tf_op jit(solution)/shard_map/ppermute | solution.py:364
  99.4 11.0 %collective-permute-start.7 = (f32[8,512]{1,0:T(8,128)S(1)}, f32[8,512]{1,0:T(8,128)S(1)}, u32[]{:S(2)}, u32[]{:S(2)}) collective-permute-start(f32[8,512]{1,0:T(8,128)S(1)} %get-tuple-element.39), channel_id=1, source_target_pairs={{0,248},{1,255},{2,254},{3,253},{4,252},{5,251},{6,250},{7,249},{8... | collective-permute-start | bytes 49160 | tf_op jit(solution)/shard_map/ppermute | solution.py:364
  101.2 9.1 %collective-permute-start.9 = (f32[8,512]{1,0:T(8,128)S(1)}, f32[8,512]{1,0:T(8,128)S(1)}, u32[]{:S(2)}, u32[]{:S(2)}) collective-permute-start(f32[8,512]{1,0:T(8,128)S(1)} %get-tuple-element.38), channel_id=1, source_target_pairs={{131,133},{130,134},{129,135}} | collective-permute-start | bytes 49160 | tf_op jit(solution)/shard_map/ppermute | solution.py:364
  146.9 54.6 %all-to-all-start.3 = ((f32[32,2,24,128]{3,2,1,0:T(8,128)}), f32[32,2,24,128]{3,2,1,0:T(8,128)S(1)}, u32[]{:S(2)}, u32[]{:S(2)}) async-start(f32[32,2,24,128]{3,2,1,0:T(8,128)} %shard_map.164), calls=%async_computation.3 | async-start | bytes 1572864 | tf_op jit(solution)/shard_map/all_to_all | solution.py:368
  151.8 44.8 %collective-permute-start.13 = (f32[24,64,128]{2,1,0:T(8,128)S(1)}, f32[24,64,128]{2,1,0:T(8,128)S(1)}, u32[]{:S(2)}, u32[]{:S(2)}) collective-permute-start(f32[24,64,128]{2,1,0:T(8,128)S(1)} %copy-done.22), channel_id=1, source_target_pairs={{0,8},{8,16},{16,24},{24,32},{32,40},{40,48},{48,56},{56,64},{64,7... | collective-permute-start | bytes 2359304 | tf_op jit(solution)/shard_map/ppermute | solution.py:360
  153.1 5.8 %collective-permute-start.15 = (f32[24,24,128]{2,1,0:T(8,128)S(1)}, f32[24,24,128]{2,1,0:T(8,128)S(1)}, u32[]{:S(2)}, u32[]{:S(2)}) collective-permute-start(f32[24,24,128]{2,1,0:T(8,128)S(1)} %copy-done.24), channel_id=1, source_target_pairs={{0,1},{1,2},{2,3},{3,4},{4,5},{5,6},{6,7},{7,0},{8,9},{9,10},{10,1... | collective-permute-start | bytes 884744 | tf_op jit(solution)/shard_map/ppermute | solution.py:360
  155.2 6.8 %collective-permute-start.14 = (f32[24,24,128]{2,1,0:T(8,128)S(1)}, f32[24,24,128]{2,1,0:T(8,128)S(1)}, u32[]{:S(2)}, u32[]{:S(2)}) collective-permute-start(f32[24,24,128]{2,1,0:T(8,128)S(1)} %copy-done.23), channel_id=1, source_target_pairs={{0,1},{1,2},{2,3},{3,4},{4,5},{5,6},{6,7},{7,0},{8,9},{9,10},{10,1... | collective-permute-start | bytes 884744 | tf_op jit(solution)/shard_map/ppermute | solution.py:360
  158.9 37.8 %collective-permute-start.16 = (f32[24,24,128]{2,1,0:T(8,128)S(1)}, f32[24,24,128]{2,1,0:T(8,128)S(1)}, u32[]{:S(2)}, u32[]{:S(2)}) collective-permute-start(f32[24,24,128]{2,1,0:T(8,128)S(1)} %collective-permute-done.15), channel_id=1, source_target_pairs={{0,8},{8,16},{16,24},{24,32},{32,40},{40,48},{48,56},{56,64},{64,7... | collective-permute-start | bytes 884744 | tf_op jit(solution)/shard_map/ppermute | solution.py:360
  162.0 34.6 %copy-start.14 = (f32[24,24,128]{2,1,0:T(8,128)}, f32[24,24,128]{2,1,0:T(8,128)S(1)}, u32[]{:S(2)}) copy-start(f32[24,24,128]{2,1,0:T(8,128)S(1)} %collective-permute-done.14.side) | copy-start | bytes 884740
  200.3 40.9 %collective-permute-start.18 = (f32[24,64,128]{2,1,0:T(8,128)}, f32[24,64,128]{2,1,0:T(8,128)S(1)}, u32[]{:S(2)}, u32[]{:S(2)}) collective-permute-start(f32[24,64,128]{2,1,0:T(8,128)} %get-tuple-element.36.oc_own), channel_id=1, source_target_pairs={{0,248},{8,0},{16,8},{24,16},{32,24},{40,32},{48,40},{56,48},{64,5... | collective-permute-start | bytes 2359304 | tf_op jit(solution)/shard_map/ppermute | solution.py:360
  205.3 42.3 %collective-permute-start.11 = (f32[24,64,128]{2,1,0:T(8,128)}, f32[24,64,128]{2,1,0:T(8,128)S(1)}, u32[]{:S(2)}, u32[]{:S(2)}) collective-permute-start(f32[24,64,128]{2,1,0:T(8,128)} %get-tuple-element.19.mu_own), channel_id=1, source_target_pairs={{0,248},{8,0},{16,8},{24,16},{32,24},{40,32},{48,40},{56,48},{64,5... | collective-permute-start | bytes 2359304 | tf_op jit(solution)/shard_map/ppermute | solution.py:360
  206.6 7.1 %collective-permute-start.17 = (f32[24,24,128]{2,1,0:T(8,128)}, f32[24,24,128]{2,1,0:T(8,128)S(1)}, u32[]{:S(2)}, u32[]{:S(2)}) collective-permute-start(f32[24,24,128]{2,1,0:T(8,128)} %get-tuple-element.37), channel_id=1, source_target_pairs={{0,7},{1,0},{2,1},{3,2},{4,3},{5,4},{6,5},{7,6},{8,15},{9,8},{10,9... | collective-permute-start | bytes 884744 | tf_op jit(solution)/shard_map/ppermute | solution.py:360
  208.6 8.3 %collective-permute-start.10 = (f32[24,24,128]{2,1,0:T(8,128)}, f32[24,24,128]{2,1,0:T(8,128)S(1)}, u32[]{:S(2)}, u32[]{:S(2)}) collective-permute-start(f32[24,24,128]{2,1,0:T(8,128)} %get-tuple-element.31), channel_id=1, source_target_pairs={{0,7},{1,0},{2,1},{3,2},{4,3},{5,4},{6,5},{7,6},{8,15},{9,8},{10,9... | collective-permute-start | bytes 884744 | tf_op jit(solution)/shard_map/ppermute | solution.py:360
  213.7 27.5 %collective-permute-start.19 = (f32[24,24,128]{2,1,0:T(8,128)S(1)}, f32[24,24,128]{2,1,0:T(8,128)S(1)}, u32[]{:S(2)}, u32[]{:S(2)}) collective-permute-start(f32[24,24,128]{2,1,0:T(8,128)S(1)} %collective-permute-done.17.oc_side), channel_id=1, source_target_pairs={{0,248},{8,0},{16,8},{24,16},{32,24},{40,32},{48,40},{56,48},{64,5... | collective-permute-start | bytes 884744 | tf_op jit(solution)/shard_map/ppermute | solution.py:360
  216.9 30.7 %collective-permute-start.12 = (f32[24,24,128]{2,1,0:T(8,128)S(1)}, f32[24,24,128]{2,1,0:T(8,128)S(1)}, u32[]{:S(2)}, u32[]{:S(2)}) collective-permute-start(f32[24,24,128]{2,1,0:T(8,128)S(1)} %collective-permute-done.10.mu_side), channel_id=1, source_target_pairs={{0,248},{8,0},{16,8},{24,16},{32,24},{40,32},{48,40},{56,48},{64,5... | collective-permute-start | bytes 884744 | tf_op jit(solution)/shard_map/ppermute | solution.py:360
  (24 other events, 148.3 us)

commit v2 on v1

v2 whole, which is shorter than its diff:
```python
import functools

import jax
import jax.numpy as jnp
import numpy as np
from jax import lax
from jax.experimental import pallas as pl
from jax.experimental.pallas import tpu as pltpu
from jax.sharding import PartitionSpec as P

NX, NY, NZ = 768, 512, 128
STEP = 8
PX, PY = 32, 8
CX, CY = NX // PX, NY // PY
OV = 24
KX = NX // PY
F32 = jnp.float32
BF16 = jnp.bfloat16
SPECIAL = 16
RATE = 0.2
GRADIENT = 0.1
COUPLING = 1.5

VM = pl.BlockSpec(memory_space=pltpu.VMEM)
SM = pl.BlockSpec(memory_space=pltpu.SMEM)


def halves(array):
    high = np.asarray(array, np.float32).astype(jnp.bfloat16)
    low = (np.asarray(array, np.float64) - high.astype(np.float64)).astype(jnp.bfloat16)
    return high, low


def slot_wave(p, h):
    if h == 0:
        return 4 * p + 1
    return 4 * p + 2 if p < 16 else 4 * p


def depth_tables():
    z = np.arange(NZ)
    forward = np.zeros((NZ, NZ))
    inverse = np.zeros((NZ, NZ))
    total = NX * NY * NZ
    for h in range(2):
        for p in range(PX):
            row_re, row_im = h * 64 + p, h * 64 + 32 + p
            wave = slot_wave(p, h)
            cosine = np.cos(2 * np.pi * ((wave * z) % NZ) / NZ)
            sine = np.sin(2 * np.pi * ((wave * z) % NZ) / NZ)
            if p == SPECIAL and h == 1:
                forward[row_re], forward[row_im] = 1.0, (-1.0) ** z
                inverse[row_re], inverse[row_im] = 1.0 / total, (-1.0) ** z / total
            else:
                forward[row_re], forward[row_im] = cosine, -sine
                inverse[row_re], inverse[row_im] = 2 * cosine / total, -2 * sine / total
    return forward, inverse


def wave_rows(count, step, length):
    angle = 2 * np.pi * ((step * np.arange(count)[:, None] * np.arange(length)[None]) % length) / length
    return np.stack([np.cos(angle), np.sin(angle)]).astype(np.float32)


def column_tables():
    k = np.arange(NY)
    angle = 2 * np.pi * ((k[:, None] * k[None]) % NY) / NY
    return halves(np.concatenate([np.cos(angle), np.sin(angle)], axis=1))


def mirror_tables():
    rows = np.zeros((KX, KX), np.float32)
    for j in range(1, KX):
        rows[j, KX - j] = 1.0
    lanes = np.zeros((NY, NY), np.float32)
    for k in range(NY):
        lanes[(NY - k) % NY, k] = 1.0
    return rows.astype(jnp.bfloat16), lanes.astype(jnp.bfloat16)


def split(value):
    high = value.astype(BF16)
    return high, (value - high.astype(F32)).astype(BF16)


def dot(a, b):
    return jnp.dot(a, b, preferred_element_type=F32)


def dot3(a, b):
    return dot(a[0], b[0]) + dot(a[0], b[1]) + dot(a[1], b[0])


def turn(value):
    return pltpu.roll(value, 64, axis=value.ndim - 1)


def low_lanes(shape):
    return lax.broadcasted_iota(jnp.int32, shape, len(shape) - 1) < 64


def call(kernel, outs, specs, args, scratch=(), **params):
    return pl.pallas_call(
        kernel,
        out_shape=outs,
        in_specs=specs,
        out_specs=jax.tree.map(lambda unused: VM, outs),
        scratch_shapes=scratch,
        compiler_params=pltpu.CompilerParams(vmem_limit_bytes=60 * 1024 * 1024, **params),
    )(*args)


def shaped(*shape, dtype=F32):
    return jax.ShapeDtypeStruct(shape, dtype)


def place_kernel(start, ids, misfit, eta, field, cover):
    field[...] = jnp.zeros_like(field)
    cover[...] = jnp.zeros_like(cover)
    for b in range(eta.shape[0]):
        weight = misfit[ids[b]]
        sx = start[0, b]
        sy = pl.multiple_of(start[1, b], 8)

        def body(i, unused):
            value = eta[b, i]
            square = value * value
            rows = pl.ds(sy, 32)
            field[sx + i, rows, :] = field[sx + i, rows, :] + weight * square
            cover[sx + i, rows, :] = cover[sx + i, rows, :] + square
            return unused

        lax.fori_loop(0, 32, body, 0, unroll=4)


MESH = pl.DeviceIdType.MESH
CUT_X = ((0, 12), (12, 36), (36, 48))
CUT_Y = ((0, 8), (8, 72), (72, 88))
LAND_X = ((12, 24), (0, 24), (0, 12))
LAND_Y = ((56, 64), (0, 64), (0, 16))
TAKE_X = ((0, 12), (0, 24), (12, 24))
TAKE_Y = ((0, 16), (0, 64), (56, 64))
GIVE_X = ((36, 48), (12, 36), (0, 12))
GIVE_Y = ((72, 88), (8, 72), (0, 8))
AROUND = [(a, b) for a, b in ((0, 1), (2, 1), (1, 0), (1, 2), (0, 0), (0, 2), (2, 0), (2, 2))]


def box(ref, x, y):
    return ref.at[pl.ds(x[0], x[1] - x[0]), pl.ds(y[0], y[1] - y[0])]


def wrap(value, count):
    return (value + count) % count


def push(source, target, send, receive, p, q):
    return pltpu.make_async_remote_copy(
        src_ref=source, dst_ref=target, send_sem=send, recv_sem=receive, device_id=(p, q), device_id_type=MESH
    )


def drain(ref, semaphore):
    pltpu.make_async_copy(ref, ref, semaphore).wait()


def mega_kernel(
    field, cover, green, coarse, fine, wave_h, wave_l, back_h, back_l, table_h, table_l, row_flip, lane_flip,
    mu_window, oc_window,
    grid, s1, r1, y1, t1, y2, t2, s2, r2, cos_h, cos_l, sin_h, sin_l,
    near, far, extra, near_row, far_row, extra_row, gs, gx, work_h, work_l, one_h, two_h, potential, occupancy,
    land_e, land_o, halo_send, halo_recv, green_send, green_recv, px_send, px_recv, py_send, py_recv,
):
    p, q = lax.axis_index("px"), lax.axis_index("py")
    upper_half = p // 16
    far_to = 31 - p + (1 - upper_half) - 16 * (1 - (p + 31) // 32)
    far_from = 31 - p + upper_half - 16 * upper_half * (1 - (p + 15) // 32)
    flip, flip_row = 7 - q, (8 - q) % 8

    barrier = pltpu.get_barrier_semaphore()

    def greet(a, b):
        pl.semaphore_signal(barrier, inc=1, device_id=(a, b), device_id_type=MESH)

    @pl.loop(1, PX)
    def _(j):
        greet((p + j) % PX, q)

    @pl.loop(1, PY)
    def _(j):
        greet(p, (q + j) % PY)

    for a in (-1, 1):
        for b in (-1, 1):
            greet(wrap(p + a, PX), wrap(q + b, PY))
    greet(31 - p, flip)
    greet(31 - p, flip_row)
    greet(far_from, flip)
    greet(far_from, flip_row)
    pl.semaphore_wait(barrier, (PX - 1) + (PY - 1) + 8)

    def scatter(source, lands, group):
        copies = []
        for n, (a, b) in enumerate(AROUND):
            copy = push(
                box(source, CUT_X[a], CUT_Y[b]), lands[n], halo_send.at[group, n], halo_recv.at[group, n],
                wrap(p + a - 1, PX), wrap(q + b - 1, PY),
            )
            copy.start()
            copies.append(copy)
        return copies

    def collect(source, lands, copies, total):
        total[...] = box(source, CUT_X[1], CUT_Y[1])[...]
        for n, (a, b) in enumerate(AROUND):
            copies[n].wait_recv()
            part = box(total, LAND_X[a], LAND_Y[b])
            part[...] = part[...] + lands[n][...]

    def spread(source, window, group):
        copies = []
        for n, (a, b) in enumerate(AROUND):
            copy = push(
                box(source, TAKE_X[a], TAKE_Y[b]), box(window, GIVE_X[a], GIVE_Y[b]),
                halo_send.at[group, n], halo_recv.at[group, n], wrap(p + a - 1, PX), wrap(q + b - 1, PY),
            )
            copy.start()
            copies.append(copy)
        box(window, CUT_X[1], CUT_Y[1])[...] = source[...]
        return copies

    pending = []
    first = scatter(field, land_e, 0)
    pending += first

    greens = [
        push(green.at[3], near, green_send.at[0], green_recv.at[0], 31 - p, flip),
        push(green.at[2 * upper_half], far, green_send.at[1], green_recv.at[1], far_to, flip),
        push(green.at[3, pl.ds(0, 8)], near_row, green_send.at[2], green_recv.at[2], 31 - p, flip_row),
        push(green.at[2 * upper_half, pl.ds(0, 8)], far_row, green_send.at[3], green_recv.at[3], far_to, flip_row),
    ]
    for copy in greens:
        copy.start()
    pending += greens

    def extra_copy(a, b):
        return push(green.at[0], extra, green_send.at[4], green_recv.at[4], a, b)

    def extra_row_copy():
        return push(green.at[0, pl.ds(0, 8)], extra_row, green_send.at[5], green_recv.at[5], SPECIAL, flip_row)

    sends_extra = ((p == 0) | (p == SPECIAL)) & (q < 4)
    sends_row = (p == SPECIAL) & (q > 0) & (q < 4)
    extra_to = q + (p // SPECIAL) * (flip - q)

    @pl.when(sends_extra)
    def _():
        extra_copy(SPECIAL, extra_to).start()

    @pl.when(sends_row)
    def _():
        extra_row_copy().start()

    fine_c, fine_s = fine[0], fine[1]

    def table_body(k, unused):
        coarse_c, coarse_s = coarse[0, pl.ds(k, 1), :], coarse[1, pl.ds(k, 1), :]
        rows = pl.ds(pl.multiple_of(32 * k, 32), 32)
        cos_h[rows, :], cos_l[rows, :] = split(coarse_c * fine_c - coarse_s * fine_s)
        sin_h[rows, :], sin_l[rows, :] = split(coarse_s * fine_c + coarse_c * fine_s)
        return unused

    lax.fori_loop(0, NX // 32, table_body, 0)

    collect(field, land_e, first, grid)

    keep = low_lanes((PX, 128))
    nt = (((1,), (1,)), ((), ()))
    for h in range(2):
        waves = (wave_h[64 * h : 64 * h + 64], wave_l[64 * h : 64 * h + 64])
        for group in range(CX // 4):
            rows = split(grid[4 * group : 4 * group + 4].reshape(256, NZ))
            spectrum = (
                lax.dot_general(waves[0], rows[0], nt, preferred_element_type=F32)
                + lax.dot_general(waves[0], rows[1], nt, preferred_element_type=F32)
                + lax.dot_general(waves[1], rows[0], nt, preferred_element_type=F32)
            )
            for tile in range(2):
                real = spectrum[0:32, 128 * tile : 128 * tile + 128]
                imag = spectrum[32:64, 128 * tile : 128 * tile + 128]
                x = 4 * group + 2 * tile
                s1.at[h][pl.ds(x, PX, stride=24), :] = jnp.where(keep, real, turn(imag))
                s1.at[h][pl.ds(x + 1, PX, stride=24), :] = jnp.where(keep, turn(real), imag)

        @pl.loop(1, PX)
        def _(j):
            to = (p + j) % PX
            rows = pl.ds(pl.multiple_of(24 * to, 8), 24)
            here = pl.ds(pl.multiple_of(24 * p, 8), 24)
            push(s1.at[h, rows], r1.at[h, here], px_send.at[0, h], px_recv.at[0, h], to, q).start()

        here = pl.ds(pl.multiple_of(24 * p, 8), 24)
        r1[h, here, :] = s1[h, here, :]

    second = scatter(cover, land_o, 1)
    pending += second

    keep = low_lanes((KX, 128))
    special = p == SPECIAL
    most = 31 * 24
    for h in range(2):
        drain(r1.at[h, pl.ds(0, most)], px_recv.at[0, h])
        high, low = split(r1[h])
        both_parts = jnp.concatenate([high, low], axis=1)
        one_h[...] = both_parts

        def rows_body(k, unused):
            rows = pl.ds(pl.multiple_of(KX * k, KX), KX)
            data = one_h[...]
            cosine = dot(cos_h[rows, :], data)
            cosine = cosine[:, :128] + cosine[:, 128:] + dot(cos_l[rows, :], data[:, :128])
            sine = dot(sin_h[rows, :], data)
            sine = sine[:, :128] + sine[:, 128:] + dot(sin_l[rows, :], data[:, :128])
            turned = turn(sine)
            value = jnp.where(keep, cosine + turned, cosine - turned)
            if h == 1:
                below = jnp.where(keep, cosine, -turned)
                above = jnp.where(keep, turn(cosine), -sine)
                parted = jnp.where(k < 4, below, above)
                top = (lax.broadcasted_iota(jnp.int32, (KX, 128), 0) == 0) & (k % 4 == 0)
                value = jnp.where(special & jnp.logical_not(top), parted, jnp.where(special, cosine, value))
            y1[h, k] = value

            @pl.when(k != q)
            def _():
                push(y1.at[h, k], t1.at[h, q], py_send.at[0, h], py_recv.at[0, h], p, k).start()

            return unused

        lax.fori_loop(0, PY, rows_body, 0)
        t1[h, q] = y1[h, q]

    for copy in greens:
        copy.wait_recv()

    @pl.when(p == SPECIAL)
    def _():
        extra_copy(SPECIAL, extra_to).wait_recv()

    @pl.when((p == SPECIAL) & (q > 4))
    def _():
        extra_row_copy().wait_recv()

    flips = row_flip[...]
    lanes_flip = lane_flip[...]

    def permute(value):
        high, low = split(value)
        return dot(high, lanes_flip) + dot(low, lanes_flip)

    def mirror(plane, row):
        high, low = split(plane)
        turned = dot(flips, high) + dot(flips, low)
        top = lax.broadcasted_iota(jnp.int32, turned.shape, 0) == 0
        return permute(jnp.where(top, jnp.broadcast_to(row, turned.shape), turned))

    upper = special & (q >= 4)
    lower = special & (q < 4)
    gs[0] = 0.5 * (green[1] + mirror(near[...], near_row[0:1]))
    base = jnp.where(p < 16, green[2], jnp.where(lower, extra[...], green[0]))
    plane = jnp.where(upper, extra[...], far[...])
    row = jnp.where(upper, extra_row[0:1], far_row[0:1])
    half = 0.5 * (base + mirror(plane, row))
    packed_rows = jnp.concatenate(
        [jnp.broadcast_to(far_row[0:1], (8, NY)), jnp.broadcast_to(green[0, 0:1], (8, NY))], axis=0
    )
    packed_rows = 0.5 * (packed_rows + permute(packed_rows))
    packed = special & (q % 4 == 0)
    top = (lax.broadcasted_iota(jnp.int32, (KX, NY), 0) == 0) & packed
    gs[1] = jnp.where(top, jnp.broadcast_to(packed_rows[0:1], (KX, NY)), half)
    gx[...] = packed_rows[8:16]

    tables = (table_h[...], table_l[...])
    for h in range(2):
        drain(t1.at[h, pl.ds(0, PY - 1)], py_recv.at[0, h])
        for tile in range(4):
            even, odd = t1[h, 2 * tile], t1[h, 2 * tile + 1]
            lanes = slice(128 * tile, 128 * tile + 128)
            work_h[0:96, lanes], work_l[0:96, lanes] = split(jnp.where(keep, even, turn(odd)))
            work_h[96:192, lanes], work_l[96:192, lanes] = split(jnp.where(keep, turn(even), odd))
        wave = dot3((work_h[0:192], work_l[0:192]), tables)
        re_c, re_s = wave[0:96, :NY], wave[0:96, NY:]
        im_c, im_s = wave[96:192, :NY], wave[96:192, NY:]
        real, imag = re_c + im_s, im_c - re_s
        if h == 1:
            real, imag = jnp.where(top, re_c, real), jnp.where(top, -re_s, imag)
            fix = gx[...]
            work_h[192:200], work_l[192:200] = split(fix * im_c[0:8])
            work_h[200:208], work_l[200:208] = split(fix * -im_s[0:8])
        work_h[0:96], work_l[0:96] = split(gs[h] * real)
        work_h[96:192], work_l[96:192] = split(gs[h] * imag)
        used = slice(0, 208 if h == 1 else 192)
        wave = dot3((work_h[used], work_l[used]), tables)
        real = wave[0:96, :NY] - wave[96:192, NY:]
        imag = wave[96:192, :NY] + wave[0:96, NY:]
        if h == 1:
            fix = wave[192:200, :NY] - wave[200:208, NY:]
            imag = jnp.where(top, jnp.broadcast_to(fix[0:1], (KX, NY)), imag)
        for tile in range(4):
            lanes = slice(128 * tile, 128 * tile + 128)
            re, im = real[:, lanes], imag[:, lanes]
            y2[h, 2 * tile] = jnp.where(keep, re, turn(im))
            y2[h, 2 * tile + 1] = jnp.where(keep, turn(re), im)

        @pl.loop(1, PY)
        def _(j):
            to = (q + j) % PY
            push(y2.at[h, to], t2.at[h, q], py_send.at[1, h], py_recv.at[1, h], p, to).start()

        t2[h, q] = y2[h, q]

    collect(cover, land_o, second, occupancy)
    third = spread(occupancy, oc_window, 2)
    pending += third

    for h in range(2):
        drain(t2.at[h, pl.ds(0, PY - 1)], py_recv.at[1, h])
        for k in range(PY):
            value = t2[h, k]
            turned = turn(value)
            one = value
            two = jnp.where(keep, -turned, turned)
            if h == 1:
                if k < 4:
                    one_s, two_s = jnp.where(keep, 2.0 * value, 0.0), jnp.where(keep, -2.0 * turned, 0.0)
                else:
                    one_s, two_s = jnp.where(keep, 0.0, 2.0 * turned), jnp.where(keep, 0.0, -2.0 * value)
                if k % 4 == 0:
                    row_zero = lax.broadcasted_iota(jnp.int32, (KX, 128), 0) == 0
                    one_s, two_s = jnp.where(row_zero, value, one_s), jnp.where(row_zero, 0.0, two_s)
                one, two = jnp.where(special, one_s, one), jnp.where(special, two_s, two)
            rows = slice(KX * k, KX * k + KX)
            one_h[rows, 0:128], one_h[rows, 128:256] = split(one)
            two_h[rows, 0:128], two_h[rows, 128:256] = split(two)

        def unrows_body(k, unused):
            rows = pl.ds(pl.multiple_of(KX * k, KX), KX)
            one, two = one_h[...], two_h[...]
            result = dot(cos_h[rows, :], one) + dot(sin_h[rows, :], two)
            result = result[:, :128] + result[:, 128:] + dot(cos_l[rows, :], one[:, :128]) + dot(sin_l[rows, :], two[:, :128])
            s2[h, rows, :] = result
            for i in range(4):
                to = 4 * k + i

                @pl.when(to != p)
                def _():
                    part = pl.ds(pl.multiple_of(24 * to, 8), 24)
                    here = pl.ds(pl.multiple_of(24 * p, 8), 24)
                    push(s2.at[h, part], r2.at[h, here], px_send.at[1, h], px_recv.at[1, h], to, q).start()

            return unused

        lax.fori_loop(0, 8, unrows_body, 0)
        here = pl.ds(pl.multiple_of(24 * p, 8), 24)
        r2[h, here, :] = s2[h, here, :]

    keep = low_lanes((PX, 128))
    for h in range(2):
        drain(r2.at[h, pl.ds(0, most)], px_recv.at[1, h])
        waves = (back_h[64 * h : 64 * h + 64], back_l[64 * h : 64 * h + 64])
        for tile in range(CX // 2):
            x = 2 * tile
            even = r2.at[h][pl.ds(x, PX, stride=24), :]
            odd = r2.at[h][pl.ds(x + 1, PX, stride=24), :]
            parts = [jnp.where(keep, even, turn(odd)), jnp.where(keep, turn(even), odd)]
            block = split(jnp.concatenate(parts, axis=0).T)
            value = dot3(block, waves).reshape(2, CY, NZ)
            if h == 0:
                potential[x : x + 2] = value
            else:
                potential[x : x + 2] = potential[x : x + 2] + value

    fourth = spread(potential, mu_window, 3)
    pending += fourth
    for copy in third + fourth:
        copy.wait_recv()

    for copy in pending:
        copy.wait_send()

    @pl.when(sends_extra)
    def _():
        extra_copy(SPECIAL, extra_to).wait_send()

    @pl.when(sends_row)
    def _():
        extra_row_copy().wait_send()

    for h in range(2):
        drain(s1.at[h, pl.ds(0, most)], px_send.at[0, h])
        drain(s2.at[h, pl.ds(0, most)], px_send.at[1, h])
        drain(y1.at[h, pl.ds(0, PY - 1)], py_send.at[0, h])
        drain(y2.at[h, pl.ds(0, PY - 1)], py_send.at[1, h])


def update_kernel(start, ids, misfit, eta, field, cover, out, potential):
    potential[...] = field[:CX, :CY]
    sublane = lax.broadcasted_iota(jnp.int32, (32, NZ), 0)
    for b in range(eta.shape[0]):
        weight = misfit[ids[b]]
        sx = start[0, b]
        sy = pl.multiple_of(start[1, b], 8)

        def body(i, unused):
            value = eta[b, i]
            before = jnp.where(i > 0, eta[b, jnp.maximum(i - 1, 0)], 0.0)
            after = jnp.where(i < 31, eta[b, jnp.minimum(i + 1, 31)], 0.0)
            above = jnp.where(sublane == 0, 0.0, pltpu.roll(value, 1, axis=0))
            below = jnp.where(sublane == 31, 0.0, pltpu.roll(value, 31, axis=0))
            lap = before + after + above + below + pltpu.roll(value, 1, axis=1) + pltpu.roll(value, 127, axis=1) - 6.0 * value
            mu = field[sx + i, pl.ds(sy, 32), :]
            total = cover[sx + i, pl.ds(sy, 32), :]
            square = value * value
            force = value * square - value + 2.0 * COUPLING * value * (total - square)
            force = force - GRADIENT * lap + 2.0 * weight * value * mu
            out[b, i] = value - RATE * force
            return unused

        lax.fori_loop(0, 32, body, 0, unroll=2)


def on_device(eta, corners, grain_ids, misfit, green):
    p, q = lax.axis_index("px"), lax.axis_index("py")
    start = jnp.stack([corners[:, 0] * STEP - p * CX, corners[:, 1] * STEP - q * CY]).astype(jnp.int32)
    forward, inverse = depth_tables()
    coarse, fine = wave_rows(24, 32, NX), wave_rows(32, 1, NX)
    patch = shaped(CX + OV, CY + OV, NZ)
    field, cover = call(place_kernel, [patch, patch], [SM, SM, SM, VM], (start, grain_ids, misfit, eta))

    def lands():
        return [
            pltpu.VMEM((CUT_X[a][1] - CUT_X[a][0], CUT_Y[b][1] - CUT_Y[b][0], NZ), F32) for a, b in AROUND
        ]

    dma = pltpu.SemaphoreType.DMA
    scratch = [
        pltpu.VMEM((CX, CY, NZ), F32),
        pltpu.VMEM((2, NX, 128), F32),
        pltpu.VMEM((2, NX, 128), F32),
        *[pltpu.VMEM((2, PY, KX, 128), F32)] * 4,
        pltpu.VMEM((2, NX, 128), F32),
        pltpu.VMEM((2, NX, 128), F32),
        *[pltpu.VMEM((NX, NX), BF16)] * 4,
        *[pltpu.VMEM((KX, NY), F32)] * 3,
        *[pltpu.VMEM((8, NY), F32)] * 3,
        pltpu.VMEM((2, KX, NY), F32),
        pltpu.VMEM((8, NY), F32),
        *[pltpu.VMEM((208, NY), BF16)] * 2,
        *[pltpu.VMEM((NX, 256), BF16)] * 2,
        pltpu.VMEM((CX, CY, NZ), F32),
        pltpu.VMEM((CX, CY, NZ), F32),
        lands(),
        lands(),
        dma((4, 8)),
        dma((4, 8)),
        dma((6,)),
        dma((6,)),
        *[dma((2, 2))] * 4,
    ]
    mu, total = call(
        mega_kernel,
        [patch, patch],
        [VM] * 13,
        (field, cover, green, coarse, fine, *halves(forward), *halves(inverse), *column_tables(), *mirror_tables()),
        scratch=scratch,
        collective_id=0,
        has_side_effects=True,
    )
    eta_next, potential = call(
        update_kernel,
        [shaped(*eta.shape), shaped(CX, CY, NZ)],
        [SM] * 3 + [VM] * 3,
        (start, grain_ids, misfit, eta, mu, total),
    )
    return eta_next, potential


def solution(mesh):
    in_specs = (P(("px", "py"), None, None, None), P(("px", "py"), None), P(("px", "py")), P(), P("px", "py", None))
    out_specs = (P(("px", "py"), None, None, None), P("px", "py", None))
    return jax.shard_map(on_device, mesh=mesh, in_specs=in_specs, out_specs=out_specs, check_vma=False)
```

time: 260 us -> 147 us (0.57)
  waiting for transfers between devices: 128 us -> 0 us
  Pallas kernels: 50.5 us -> 145 us
  starting transfers between devices: 53 us -> 0 us
  blocking collectives: 17.8 us -> 0 us
  local copies, waits for them, and re-layouts: 7.55 us -> 0 us
    ppermute x20 -> x0, waiting for transfers between devices: 114 us -> none  [the longest x14 103 us: shift(): lax.ppermute(value, axis, [(i, (i + by) % peers) for i in range(peers)])]
    pallas_call x10 -> x3, Pallas kernels: 50.5 us -> 145 us  [call(): pl.pallas_call(kernel, out_shape=outs, in_specs=specs, out_specs=jax.tree...]
    ppermute x20 -> x0, starting transfers between devices: 32.7 us -> none  [the longest x14 17.6 us: shift(): lax.ppermute(value, axis, [(i, (i + by) % peers) for i in range(peers)])]
    all_to_all x3 -> x0, starting transfers between devices: 20.3 us -> none  [exchange(): return lax.all_to_all(value, axis, split_axis=0, concat_axis=0, tiled=True)]
    all_to_all x1 -> x0, blocking collectives: 17.8 us -> none  [exchange(): return lax.all_to_all(value, axis, split_axis=0, concat_axis=0, tiled=True)]
    all_to_all x3 -> x0, waiting for transfers between devices: 13.8 us -> none  [exchange(): return lax.all_to_all(value, axis, split_axis=0, concat_axis=0, tiled=True)]
    unnamed x50 -> x0, local copies, waits for them, and re-layouts: 7.52 us -> none
  transfers between devices with their start and end apart: 23 -> 0, of which waited for: 14 -> 0; matrix products, arithmetic and copies ran while one was open for 0% -> 0% of each run, Pallas kernels for 5% -> 0%
where the time goes in v2:
time: 147 us
  Pallas kernels  145 us (99%)
    pallas_call x3, Pallas kernels, call(): pl.pallas_call(kernel, out_shape=outs, in_specs=specs, out_specs=jax.tree...  145 us

profile of v2, /device:TPU:1, one launch (start us, length us, event | category | flops | bytes accessed | tf_op | source)
XLA Modules:
  0.0 146.5 jit_solution(1755948714627104492)
XLA Ops:
  0.6 0.8 subtract_bitcast_fusion.1
  1.4 0.5 pad_add_fusion.start
  1.9 4.4 %shard_map.158 = (f32[48,88,128]{2,1,0:T(8,128)}, f32[48,88,128]{2,1,0:T(8,128)}) custom-call(s32[2,4]{1,0:T(2,128)} %pad_add_fusion.start, s32[4]{0:T(128)} %ids.3, f32[24]{0:T(128)} %misfit.3, f32[4,32,32,128]{3,2,1,0:T(8,128)} %eta.3), custom_call_target="tpu_custom_call" | custom-call | tf_op jit(solution)/shard_map/pallas_call | solution.py:103
  6.4 129.7 %shard_map.159 = (f32[48,88,128]{2,1,0:T(8,128)}, f32[48,88,128]{2,1,0:T(8,128)}) custom-call(f32[48,88,128]{2,1,0:T(8,128)} %get-tuple-element.6.field, f32[48,88,128]{2,1,0:T(8,128)} %get-tuple-element.7.cover, f32[4,96,512]{2,1,0:T(8,128)} %green.1, f32[2,24,768]{2,1,0:T(8,128)} %constant.35.clone.coarse, f32[2,32,768]{2,1,0:T(8,128)} %constant.36.clone.fine, ...), custom_call_target="tpu_custom_call" | custom-call | tf_op jit(solution)/shard_map/pallas_call | solution.py:103
  136.1 10.4 %shard_map.160 = (f32[4,32,32,128]{3,2,1,0:T(8,128)}, f32[24,64,128]{2,1,0:T(8,128)}) custom-call(s32[2,4]{1,0:T(2,128)} %pad_add_fusion.start, s32[4]{0:T(128)} %ids.3, f32[24]{0:T(128)} %misfit.3, f32[4,32,32,128]{3,2,1,0:T(8,128)} %eta.3, f32[48,88,128]{2,1,0:T(8,128)} %get-tuple-element.8.field, f32[48,88,128]{2,1,0:T(8,128)} %get-tuple-element.9.cover), custom_call_target="tpu_custom_call" | custom-call | tf_op jit(solution)/shard_map/pallas_call | solution.py:103

commit v3 on v2

--- a/solution.py
+++ b/solution.py
@@ -21,7 +21,6 @@
 GRADIENT = 0.1
 COUPLING = 1.5
 
-VM = pl.BlockSpec(memory_space=pltpu.VMEM)
 SM = pl.BlockSpec(memory_space=pltpu.SMEM)
 
 
@@ -99,45 +98,13 @@
     return lax.broadcasted_iota(jnp.int32, shape, len(shape) - 1) < 64
 
 
-def call(kernel, outs, specs, args, scratch=(), **params):
-    return pl.pallas_call(
-        kernel,
-        out_shape=outs,
-        in_specs=specs,
-        out_specs=jax.tree.map(lambda unused: VM, outs),
-        scratch_shapes=scratch,
-        compiler_params=pltpu.CompilerParams(vmem_limit_bytes=60 * 1024 * 1024, **params),
-    )(*args)
-
-
 def shaped(*shape, dtype=F32):
     return jax.ShapeDtypeStruct(shape, dtype)
-
-
-def place_kernel(start, ids, misfit, eta, field, cover):
-    field[...] = jnp.zeros_like(field)
-    cover[...] = jnp.zeros_like(cover)
-    for b in range(eta.shape[0]):
-        weight = misfit[ids[b]]
-        sx = start[0, b]
-        sy = pl.multiple_of(start[1, b], 8)
-
-        def body(i, unused):
-            value = eta[b, i]
-            square = value * value
-            rows = pl.ds(sy, 32)
-            field[sx + i, rows, :] = field[sx + i, rows, :] + weight * square
-            cover[sx + i, rows, :] = cover[sx + i, rows, :] + square
-            return unused
-
-        lax.fori_loop(0, 32, body, 0, unroll=4)
 
 
 MESH = pl.DeviceIdType.MESH
 CUT_X = ((0, 12), (12, 36), (36, 48))
 CUT_Y = ((0, 8), (8, 72), (72, 88))
-LAND_X = ((12, 24), (0, 24), (0, 12))
-LAND_Y = ((56, 64), (0, 64), (0, 16))
 TAKE_X = ((0, 12), (0, 24), (12, 24))
 TAKE_Y = ((0, 16), (0, 64), (56, 64))
 GIVE_X = ((36, 48), (12, 36), (0, 12))
@@ -164,17 +131,35 @@
 
 
 def mega_kernel(
-    field, cover, green, coarse, fine, wave_h, wave_l, back_h, back_l, table_h, table_l, row_flip, lane_flip,
-    mu_window, oc_window,
+    eta_in, field_in, cover_in, green_in, coarse_in, fine_in, wave_h_in, wave_l_in, back_h_in, back_l_in,
+    table_h_in, table_l_in, row_flip_in, lane_flip_in,
+    base_out, mu_out, oc_out,
+    green, coarse, fine, wave_h, wave_l, back_h, back_l, table_h, table_l, row_flip, lane_flip,
+    load_sem, eta_sem, out_sem, eta, result, field, cover, mu_window, oc_window,
     grid, s1, r1, y1, t1, y2, t2, s2, r2, cos_h, cos_l, sin_h, sin_l,
-    near, far, extra, near_row, far_row, extra_row, gs, gx, work_h, work_l, one_h, two_h, potential, occupancy,
-    land_e, land_o, halo_send, halo_recv, green_send, green_recv, px_send, px_recv, py_send, py_recv,
+    near, far, extra, near_row, far_row, extra_row, gs, gx, work_h, work_l, one_h, two_h, potential,
+    low_y, high_y, low_x, high_x, side_o, low_o, high_o, halo_send, halo_recv, green_send, green_recv, px_send, px_recv, py_send, py_recv,
 ):
     p, q = lax.axis_index("px"), lax.axis_index("py")
     upper_half = p // 16
     far_to = 31 - p + (1 - upper_half) - 16 * (1 - (p + 31) // 32)
     far_from = 31 - p + upper_half - 16 * upper_half * (1 - (p + 15) // 32)
     flip, flip_row = 7 - q, (8 - q) % 8
+
+    pairs = (
+        (green_in, green), (coarse_in, coarse), (fine_in, fine), (wave_h_in, wave_h), (wave_l_in, wave_l),
+        (back_h_in, back_h), (back_l_in, back_l), (table_h_in, table_h), (table_l_in, table_l),
+        (row_flip_in, row_flip), (lane_flip_in, lane_flip),
+    )
+    boxes = eta_in.shape[0]
+    patches = [
+        pltpu.make_async_copy(field_in, field, eta_sem.at[0]),
+        pltpu.make_async_copy(cover_in, cover, eta_sem.at[1]),
+        pltpu.make_async_copy(eta_in, eta, eta_sem.at[2]),
+    ]
+    loads = [pltpu.make_async_copy(source, target, load_sem.at[n]) for n, (source, target) in enumerate(pairs)]
+    for copy in patches + loads:
+        copy.start()
 
     barrier = pltpu.get_barrier_semaphore()
 
@@ -197,24 +182,6 @@
     greet(far_from, flip)
     greet(far_from, flip_row)
     pl.semaphore_wait(barrier, (PX - 1) + (PY - 1) + 8)
-
-    def scatter(source, lands, group):
-        copies = []
-        for n, (a, b) in enumerate(AROUND):
-            copy = push(
-                box(source, CUT_X[a], CUT_Y[b]), lands[n], halo_send.at[group, n], halo_recv.at[group, n],
-                wrap(p + a - 1, PX), wrap(q + b - 1, PY),
-            )
-            copy.start()
-            copies.append(copy)
-        return copies
-
-    def collect(source, lands, copies, total):
-        total[...] = box(source, CUT_X[1], CUT_Y[1])[...]
-        for n, (a, b) in enumerate(AROUND):
-            copies[n].wait_recv()
-            part = box(total, LAND_X[a], LAND_Y[b])
-            part[...] = part[...] + lands[n][...]
 
     def spread(source, window, group):
         copies = []
@@ -228,38 +195,57 @@
         box(window, CUT_X[1], CUT_Y[1])[...] = source[...]
         return copies
 
-    pending = []
-    first = scatter(field, land_e, 0)
-    pending += first
-
-    greens = [
-        push(green.at[3], near, green_send.at[0], green_recv.at[0], 31 - p, flip),
-        push(green.at[2 * upper_half], far, green_send.at[1], green_recv.at[1], far_to, flip),
-        push(green.at[3, pl.ds(0, 8)], near_row, green_send.at[2], green_recv.at[2], 31 - p, flip_row),
-        push(green.at[2 * upper_half, pl.ds(0, 8)], far_row, green_send.at[3], green_recv.at[3], far_to, flip_row),
-    ]
-    for copy in greens:
+    near_copies = [
+        push(green_in.at[3], near, green_send.at[0], green_recv.at[0], 31 - p, flip),
+        push(green_in.at[3, pl.ds(0, 8)], near_row, green_send.at[2], green_recv.at[2], 31 - p, flip_row),
+    ]
+    far_copies = [
+        push(green_in.at[2 * upper_half], far, green_send.at[1], green_recv.at[1], far_to, flip),
+        push(green_in.at[2 * upper_half, pl.ds(0, 8)], far_row, green_send.at[3], green_recv.at[3], far_to, flip_row),
+    ]
+    for copy in near_copies:
         copy.start()
-    pending += greens
+    pending = near_copies + far_copies
+    next_p, last_p, next_q, last_q = wrap(p + 1, PX), wrap(p - 1, PX), wrap(q + 1, PY), wrap(q - 1, PY)
+
+    def halo(source, target, slot, a, b):
+        copy = push(source, target, halo_send.at[0, slot], halo_recv.at[0, slot], a, b)
+        pending.append(copy)
+        return copy
+
+    patches[0].wait()
+    along_y = [
+        halo(field.at[:, pl.ds(0, 8)], low_y, 0, p, last_q),
+        halo(field.at[:, pl.ds(72, 16)], high_y, 1, p, next_q),
+    ]
+    for copy in along_y:
+        copy.start()
+    patches[1].wait()
+    side_copy = halo(cover.at[:, pl.ds(CY, OV)], side_o, 2, p, next_q)
+    side_copy.start()
+    for copy in along_y:
+        copy.wait_recv()
+    field[:, 64:72] = field[:, 64:72] + low_y[...]
+    field[:, 8:24] = field[:, 8:24] + high_y[...]
+    along_x = [
+        halo(field.at[pl.ds(0, 12), pl.ds(8, CY)], low_x, 3, last_p, q),
+        halo(field.at[pl.ds(36, 12), pl.ds(8, CY)], high_x, 4, next_p, q),
+    ]
+    for copy in along_x:
+        copy.start()
 
     def extra_copy(a, b):
-        return push(green.at[0], extra, green_send.at[4], green_recv.at[4], a, b)
+        return push(green_in.at[0], extra, green_send.at[4], green_recv.at[4], a, b)
 
     def extra_row_copy():
-        return push(green.at[0, pl.ds(0, 8)], extra_row, green_send.at[5], green_recv.at[5], SPECIAL, flip_row)
+        return push(green_in.at[0, pl.ds(0, 8)], extra_row, green_send.at[5], green_recv.at[5], SPECIAL, flip_row)
 
     sends_extra = ((p == 0) | (p == SPECIAL)) & (q < 4)
     sends_row = (p == SPECIAL) & (q > 0) & (q < 4)
     extra_to = q + (p // SPECIAL) * (flip - q)
 
-    @pl.when(sends_extra)
-    def _():
-        extra_copy(SPECIAL, extra_to).start()
-
-    @pl.when(sends_row)
-    def _():
-        extra_row_copy().start()
-
+    for copy in loads:
+        copy.wait()
     fine_c, fine_s = fine[0], fine[1]
 
     def table_body(k, unused):
@@ -271,7 +257,10 @@
 
     lax.fori_loop(0, NX // 32, table_body, 0)
 
-    collect(field, land_e, first, grid)
+    for copy in along_x:
+        copy.wait_recv()
+    grid[0:12] = field[12:24, 8:72] + high_x[...]
+    grid[12:24] = field[24:36, 8:72] + low_x[...]
 
     keep = low_lanes((PX, 128))
     nt = (((1,), (1,)), ((), ()))
@@ -301,8 +290,42 @@
         here = pl.ds(pl.multiple_of(24 * p, 8), 24)
         r1[h, here, :] = s1[h, here, :]
 
-    second = scatter(cover, land_o, 1)
-    pending += second
+    for copy in far_copies:
+        copy.start()
+
+    @pl.when(sends_extra)
+    def _():
+        extra_copy(SPECIAL, extra_to).start()
+
+    @pl.when(sends_row)
+    def _():
+        extra_row_copy().start()
+
+    side_copy.wait_recv()
+    cover[:, 0:OV] = cover[:, 0:OV] + side_o[...]
+    cover_x = [
+        halo(cover.at[pl.ds(0, 24), pl.ds(0, CY)], low_o, 5, last_p, q),
+        halo(cover.at[pl.ds(24, 24), pl.ds(0, CY)], high_o, 6, next_p, q),
+    ]
+    for copy in cover_x:
+        copy.start()
+
+    flips = row_flip[...]
+    lanes_flip = lane_flip[...]
+
+    def permute(value):
+        high, low = split(value)
+        return dot(high, lanes_flip) + dot(low, lanes_flip)
+
+    def mirror(plane, row):
+        high, low = split(plane)
+        turned = dot(flips, high) + dot(flips, low)
+        first_row = lax.broadcasted_iota(jnp.int32, turned.shape, 0) == 0
+        return permute(jnp.where(first_row, jnp.broadcast_to(row, turned.shape), turned))
+
+    for copy in near_copies:
+        copy.wait_recv()
+    gs[0] = 0.5 * (green[1] + mirror(near[...], near_row[0:1]))
 
     keep = low_lanes((KX, 128))
     special = p == SPECIAL
@@ -339,48 +362,38 @@
         lax.fori_loop(0, PY, rows_body, 0)
         t1[h, q] = y1[h, q]
 
-    for copy in greens:
-        copy.wait_recv()
-
-    @pl.when(p == SPECIAL)
-    def _():
-        extra_copy(SPECIAL, extra_to).wait_recv()
-
-    @pl.when((p == SPECIAL) & (q > 4))
-    def _():
-        extra_row_copy().wait_recv()
-
-    flips = row_flip[...]
-    lanes_flip = lane_flip[...]
-
-    def permute(value):
-        high, low = split(value)
-        return dot(high, lanes_flip) + dot(low, lanes_flip)
-
-    def mirror(plane, row):
-        high, low = split(plane)
-        turned = dot(flips, high) + dot(flips, low)
-        top = lax.broadcasted_iota(jnp.int32, turned.shape, 0) == 0
-        return permute(jnp.where(top, jnp.broadcast_to(row, turned.shape), turned))
-
-    upper = special & (q >= 4)
-    lower = special & (q < 4)
-    gs[0] = 0.5 * (green[1] + mirror(near[...], near_row[0:1]))
-    base = jnp.where(p < 16, green[2], jnp.where(lower, extra[...], green[0]))
-    plane = jnp.where(upper, extra[...], far[...])
-    row = jnp.where(upper, extra_row[0:1], far_row[0:1])
-    half = 0.5 * (base + mirror(plane, row))
-    packed_rows = jnp.concatenate(
-        [jnp.broadcast_to(far_row[0:1], (8, NY)), jnp.broadcast_to(green[0, 0:1], (8, NY))], axis=0
-    )
-    packed_rows = 0.5 * (packed_rows + permute(packed_rows))
     packed = special & (q % 4 == 0)
     top = (lax.broadcasted_iota(jnp.int32, (KX, NY), 0) == 0) & packed
-    gs[1] = jnp.where(top, jnp.broadcast_to(packed_rows[0:1], (KX, NY)), half)
-    gx[...] = packed_rows[8:16]
+
+    def second_green():
+        for copy in far_copies:
+            copy.wait_recv()
+
+        @pl.when(p == SPECIAL)
+        def _():
+            extra_copy(SPECIAL, extra_to).wait_recv()
+
+        @pl.when((p == SPECIAL) & (q > 4))
+        def _():
+            extra_row_copy().wait_recv()
+
+        upper = special & (q >= 4)
+        lower = special & (q < 4)
+        base = jnp.where(p < 16, green[2], jnp.where(lower, extra[...], green[0]))
+        plane = jnp.where(upper, extra[...], far[...])
+        row = jnp.where(upper, extra_row[0:1], far_row[0:1])
+        half = 0.5 * (base + mirror(plane, row))
+        packed_rows = jnp.concatenate(
+            [jnp.broadcast_to(far_row[0:1], (8, NY)), jnp.broadcast_to(green[0, 0:1], (8, NY))], axis=0
+        )
+        packed_rows = 0.5 * (packed_rows + permute(packed_rows))
+        gs[1] = jnp.where(top, jnp.broadcast_to(packed_rows[0:1], (KX, NY)), half)
+        gx[...] = packed_rows[8:16]
 
     tables = (table_h[...], table_l[...])
     for h in range(2):
+        if h == 1:
+            second_green()
         drain(t1.at[h, pl.ds(0, PY - 1)], py_recv.at[0, h])
         for tile in range(4):
             even, odd = t1[h, 2 * tile], t1[h, 2 * tile + 1]
@@ -418,9 +431,12 @@
 
         t2[h, q] = y2[h, q]
 
-    collect(cover, land_o, second, occupancy)
-    third = spread(occupancy, oc_window, 2)
-    pending += third
+    for copy in cover_x:
+        copy.wait_recv()
+    oc_window[0:24, 0:CY] = cover[0:24, 0:CY] + high_o[...]
+    oc_window[24:48, 0:CY] = cover[24:48, 0:CY] + low_o[...]
+    cover_y = halo(oc_window.at[:, pl.ds(0, OV)], oc_window.at[:, pl.ds(CY, OV)], 7, p, last_q)
+    cover_y.start()
 
     for h in range(2):
         drain(t2.at[h, pl.ds(0, PY - 1)], py_recv.at[1, h])
@@ -463,6 +479,31 @@
         here = pl.ds(pl.multiple_of(24 * p, 8), 24)
         r2[h, here, :] = s2[h, here, :]
 
+    cover_y.wait_recv()
+    oc_copy = pltpu.make_async_copy(oc_window, oc_out, out_sem.at[boxes])
+    oc_copy.start()
+    patches[2].wait()
+    sublane = lax.broadcasted_iota(jnp.int32, (32, NZ), 0)
+    outs = [oc_copy]
+    for b in range(boxes):
+
+        def base_body(i, unused):
+            value = eta[b, i]
+            before = jnp.where(i > 0, eta[b, jnp.maximum(i - 1, 0)], 0.0)
+            after = jnp.where(i < 31, eta[b, jnp.minimum(i + 1, 31)], 0.0)
+            above = jnp.where(sublane == 0, 0.0, pltpu.roll(value, 1, axis=0))
+            below = jnp.where(sublane == 31, 0.0, pltpu.roll(value, 31, axis=0))
+            lap = before + after + above + below + pltpu.roll(value, 1, axis=1) + pltpu.roll(value, 127, axis=1)
+            lap = lap - 6.0 * value
+            square = value * value
+            force = value * square - value - 2.0 * COUPLING * value * square - GRADIENT * lap
+            result[b, i] = value - RATE * force
+            return unused
+
+        lax.fori_loop(0, 32, base_body, 0, unroll=2)
+        outs.append(pltpu.make_async_copy(result.at[b], base_out.at[b], out_sem.at[b]))
+        outs[-1].start()
+
     keep = low_lanes((PX, 128))
     for h in range(2):
         drain(r2.at[h, pl.ds(0, most)], px_recv.at[1, h])
@@ -479,10 +520,12 @@
             else:
                 potential[x : x + 2] = potential[x : x + 2] + value
 
-    fourth = spread(potential, mu_window, 3)
-    pending += fourth
-    for copy in third + fourth:
+    around = spread(potential, mu_window, 1)
+    pending += around
+    for copy in around:
         copy.wait_recv()
+    outs.append(pltpu.make_async_copy(mu_window, mu_out, out_sem.at[boxes + 1]))
+    outs[-1].start()
 
     for copy in pending:
         copy.wait_send()
@@ -500,49 +543,78 @@
         drain(s2.at[h, pl.ds(0, most)], px_send.at[1, h])
         drain(y1.at[h, pl.ds(0, PY - 1)], py_send.at[0, h])
         drain(y2.at[h, pl.ds(0, PY - 1)], py_send.at[1, h])
-
-
-def update_kernel(start, ids, misfit, eta, field, cover, out, potential):
-    potential[...] = field[:CX, :CY]
-    sublane = lax.broadcasted_iota(jnp.int32, (32, NZ), 0)
+    for copy in outs:
+        copy.wait()
+
+
+def place_kernel(corners, ids, misfit, eta, field, cover):
+    shift_x, shift_y = lax.axis_index("px") * CX, lax.axis_index("py") * CY
+    field[...] = jnp.zeros_like(field)
+    cover[...] = jnp.zeros_like(cover)
     for b in range(eta.shape[0]):
         weight = misfit[ids[b]]
-        sx = start[0, b]
-        sy = pl.multiple_of(start[1, b], 8)
+        sx = corners[b, 0] * STEP - shift_x
+        sy = pl.multiple_of(corners[b, 1] * STEP - shift_y, 8)
 
         def body(i, unused):
             value = eta[b, i]
-            before = jnp.where(i > 0, eta[b, jnp.maximum(i - 1, 0)], 0.0)
-            after = jnp.where(i < 31, eta[b, jnp.minimum(i + 1, 31)], 0.0)
-            above = jnp.where(sublane == 0, 0.0, pltpu.roll(value, 1, axis=0))
-            below = jnp.where(sublane == 31, 0.0, pltpu.roll(value, 31, axis=0))
-            lap = before + after + above + below + pltpu.roll(value, 1, axis=1) + pltpu.roll(value, 127, axis=1) - 6.0 * value
-            mu = field[sx + i, pl.ds(sy, 32), :]
-            total = cover[sx + i, pl.ds(sy, 32), :]
             square = value * value
-            force = value * square - value + 2.0 * COUPLING * value * (total - square)
-            force = force - GRADIENT * lap + 2.0 * weight * value * mu
-            out[b, i] = value - RATE * force
+            rows = pl.ds(sy, 32)
+            field[sx + i, rows, :] = field[sx + i, rows, :] + weight * square
+            cover[sx + i, rows, :] = cover[sx + i, rows, :] + square
             return unused
 
-        lax.fori_loop(0, 32, body, 0, unroll=2)
+        lax.fori_loop(0, 32, body, 0, unroll=4)
+
+
+def final_kernel(corners, ids, misfit, eta, base, mu_window, oc_window, out, potential):
+    b = pl.program_id(0)
+    shift_x, shift_y = lax.axis_index("px") * CX, lax.axis_index("py") * CY
+
+    @pl.when(b == 0)
+    def _():
+        potential[...] = mu_window[:CX, :CY]
+
+    factor = 2.0 * RATE * misfit[ids[b]]
+    sx = corners[b, 0] * STEP - shift_x
+    sy = pl.multiple_of(corners[b, 1] * STEP - shift_y, 8)
+
+    def body(i, unused):
+        rows = pl.ds(sy, 32)
+        mu = mu_window[sx + i, rows, :]
+        total = oc_window[sx + i, rows, :]
+        out[0, i] = base[0, i] - eta[0, i] * (2.0 * RATE * COUPLING * total + factor * mu)
+        return unused
+
+    lax.fori_loop(0, 32, body, 0, unroll=4)
 
 
 def on_device(eta, corners, grain_ids, misfit, green):
-    p, q = lax.axis_index("px"), lax.axis_index("py")
-    start = jnp.stack([corners[:, 0] * STEP - p * CX, corners[:, 1] * STEP - q * CY]).astype(jnp.int32)
     forward, inverse = depth_tables()
-    coarse, fine = wave_rows(24, 32, NX), wave_rows(32, 1, NX)
-    patch = shaped(CX + OV, CY + OV, NZ)
-    field, cover = call(place_kernel, [patch, patch], [SM, SM, SM, VM], (start, grain_ids, misfit, eta))
-
-    def lands():
-        return [
-            pltpu.VMEM((CUT_X[a][1] - CUT_X[a][0], CUT_Y[b][1] - CUT_Y[b][0], NZ), F32) for a, b in AROUND
-        ]
-
+    patch = pltpu.VMEM((CX + OV, CY + OV, NZ), F32)
     dma = pltpu.SemaphoreType.DMA
+    arrays = [
+        green, wave_rows(24, 32, NX), wave_rows(32, 1, NX), *halves(forward), *halves(inverse), *column_tables(),
+        *mirror_tables(),
+    ]
+    boxes = eta.shape[0]
+    cells = shaped(CX + OV, CY + OV, NZ)
+    local = pltpu.CompilerParams(vmem_limit_bytes=32 * 1024 * 1024)
+    field, cover = pl.pallas_call(
+        place_kernel,
+        out_shape=[cells, cells],
+        in_specs=[SM] * 3 + [pl.BlockSpec(memory_space=pltpu.VMEM)],
+        out_specs=[pl.BlockSpec(memory_space=pltpu.VMEM)] * 2,
+        compiler_params=local,
+    )(corners, grain_ids, misfit, eta)
     scratch = [
+        *[pltpu.VMEM(a.shape, a.dtype) for a in arrays],
+        dma((len(arrays),)),
+        dma((3,)),
+        dma((boxes + 2,)),
+        pltpu.VMEM((boxes, 32, 32, NZ), F32),
+        pltpu.VMEM((boxes, 32, 32, NZ), F32),
+        *[patch] * 4,
         pltpu.VMEM((CX, CY, NZ), F32),
         pltpu.VMEM((2, NX, 128), F32),
         pltpu.VMEM((2, NX, 128), F32),
@@ -557,31 +629,40 @@
         *[pltpu.VMEM((208, NY), BF16)] * 2,
         *[pltpu.VMEM((NX, 256), BF16)] * 2,
         pltpu.VMEM((CX, CY, NZ), F32),
-        pltpu.VMEM((CX, CY, NZ), F32),
-        lands(),
-        lands(),
-        dma((4, 8)),
-        dma((4, 8)),
+        pltpu.VMEM((CX + OV, 8, NZ), F32),
+        pltpu.VMEM((CX + OV, 16, NZ), F32),
+        pltpu.VMEM((12, CY, NZ), F32),
+        pltpu.VMEM((12, CY, NZ), F32),
+        pltpu.VMEM((CX + OV, OV, NZ), F32),
+        pltpu.VMEM((24, CY, NZ), F32),
+        pltpu.VMEM((24, CY, NZ), F32),
+        dma((2, 8)),
+        dma((2, 8)),
         dma((6,)),
         dma((6,)),
         *[dma((2, 2))] * 4,
     ]
-    mu, total = call(
+    hbm = pl.BlockSpec(memory_space=pl.ANY)
+    base, mu, total = pl.pallas_call(
         mega_kernel,
-        [patch, patch],
-        [VM] * 13,
-        (field, cover, green, coarse, fine, *halves(forward), *halves(inverse), *column_tables(), *mirror_tables()),
-        scratch=scratch,
-        collective_id=0,
-        has_side_effects=True,
-    )
-    eta_next, potential = call(
-        update_kernel,
-        [shaped(*eta.shape), shaped(CX, CY, NZ)],
-        [SM] * 3 + [VM] * 3,
-        (start, grain_ids, misfit, eta, mu, total),
-    )
-    return eta_next, potential
+        out_shape=[shaped(*eta.shape), cells, cells],
+        in_specs=[hbm] * (3 + len(arrays)),
+        out_specs=[hbm] * 3,
+        scratch_shapes=scratch,
+        compiler_params=pltpu.CompilerParams(
+            vmem_limit_bytes=56 * 1024 * 1024, collective_id=0, has_side_effects=True
+        ),
+    )(eta, field, cover, *arrays)
+    block = pl.BlockSpec((1, 32, 32, NZ), lambda b: (b, 0, 0, 0))
+    window = pl.BlockSpec((CX + OV, CY + OV, NZ), lambda b: (0, 0, 0))
+    return pl.pallas_call(
+        final_kernel,
+        grid=(boxes,),
+        out_shape=[shaped(*eta.shape), shaped(CX, CY, NZ)],
+        in_specs=[SM] * 3 + [block, block, window, window],
+        out_specs=[block, pl.BlockSpec((CX, CY, NZ), lambda b: (0, 0, 0))],
+        compiler_params=local,
+    )(corners, grain_ids, misfit, eta, base, mu, total)
 
 
 def solution(mesh):

time: 147 us -> 134 us (0.912)
  Pallas kernels: 145 us -> 121 us
  local copies, waits for them, and re-layouts: 0 us -> 11.2 us
    pallas_call x3, Pallas kernels: 145 us -> 121 us  [the longest x1 117 us: on_device(): pl.pallas_call(mega_kernel, out_shape=[shaped(*eta.shape), cells, cells],...]
    unnamed x0 -> x23, local copies, waits for them, and re-layouts: none -> 11.2 us
where the time goes in v3:
time: 134 us; the launch traced here: 133 us
  Pallas kernels  121 us (90%)
  local copies, waits for them, and re-layouts  11.2 us (8%)
    pallas_call x1, Pallas kernels, on_device(): pl.pallas_call(mega_kernel, out_shape=[shaped(*eta.shape), cells, cells],...  117 us
    unnamed x23, local copies, waits for them, and re-layouts  11.2 us
    pallas_call x1, Pallas kernels, on_device(): pl.pallas_call(final_kernel, grid=(boxes,), out_shape=[shaped(*eta.shape)...  3.04 us

profile of v3, /device:TPU:1, one launch (start us, length us, event | category | flops | bytes accessed | tf_op | source)
XLA Modules:
  0.0 133.0 jit_solution(11976650227712905530)
XLA Ops:
  0.6 0.8 copy.18.corners
  1.4 0.0 copy-start
  1.4 1.6 %copy-done = f32[4,32,32,128]{3,2,1,0:T(8,128)S(1)} copy-done((f32[4,32,32,128]{3,2,1,0:T(8,128)S(1)}, f32[4,32,32,128]{3,2,1,0:T(8,128)}, u32[]{:S(2)}) %copy-start) | copy-done | bytes 2097176
  3.0 0.0 copy-start.7
  3.0 0.7 copy-done.7
  3.6 0.0 copy-start.9
  3.6 0.7 copy-done.9
  4.3 1.4 %shard_map.158 = (f32[48,88,128]{2,1,0:T(8,128)S(1)}, f32[48,88,128]{2,1,0:T(8,128)S(1)}) custom-call(s32[4,2]{1,0:T(4,128)S(1)} %copy.18.corners, s32[4]{0:T(128)S(1)} %copy-done.7, f32[24]{0:T(128)S(1)} %copy-done.9, f32[4,32,32,128]{3,2,1,0:T(8,128)S(1)} %copy-done), custom_call_target="tpu_custom_call" | custom-call | tf_op jit(solution)/shard_map/pallas_call | solution.py:603
  5.7 0.0 copy-start.4
  5.7 1.3 %copy-done.4 = f32[48,88,128]{2,1,0:T(8,128)} copy-done((f32[48,88,128]{2,1,0:T(8,128)}, f32[48,88,128]{2,1,0:T(8,128)S(1)}, u32[]{:S(2)}) %copy-start.4) | copy-done | bytes 2162712
  7.0 0.0 copy-start.5
  7.0 1.3 copy-done.5
  8.3 0.0 copy-start.1
  8.3 0.0 copy-start.8
  8.3 0.0 copy-start.10
  8.4 116.8 %shard_map.159 = (f32[4,32,32,128]{3,2,1,0:T(8,128)}, f32[48,88,128]{2,1,0:T(8,128)}, f32[48,88,128]{2,1,0:T(8,128)}) custom-call(f32[4,32,32,128]{3,2,1,0:T(8,128)} %eta.3, f32[48,88,128]{2,1,0:T(8,128)} %copy-done.4, f32[48,88,128]{2,1,0:T(8,128)} %copy-done.5, f32[4,96,512]{2,1,0:T(8,128)} %green_in.1, f32[2,24,768]{2,1,0:T(8,128)} %constant.20.clone.coarse_in, ...), custom_call_target="tpu_custom_call" | custom-call | tf_op jit(solution)/shard_map/pallas_call | solution.py:646
  125.1 0.0 copy-done.1
  125.1 0.0 copy-done.8
  125.1 0.0 copy-done.10
  125.2 0.0 copy-start.2
  125.2 1.6 %copy-done.2 = f32[48,88,128]{2,1,0:T(8,128)S(1)} copy-done((f32[48,88,128]{2,1,0:T(8,128)S(1)}, f32[48,88,128]{2,1,0:T(8,128)}, u32[]{:S(2)}) %copy-start.2) | copy-done | bytes 2162712
  126.8 1.6 %copy-done.3 = f32[48,88,128]{2,1,0:T(8,128)S(1)} copy-done((f32[48,88,128]{2,1,0:T(8,128)S(1)}, f32[48,88,128]{2,1,0:T(8,128)}, u32[]{:S(2)}) %copy-start.3) | copy-done | bytes 2162712
  128.4 1.6 %copy-done.6 = f32[4,32,32,128]{3,2,1,0:T(8,128)S(1)} copy-done((f32[4,32,32,128]{3,2,1,0:T(8,128)S(1)}, f32[4,32,32,128]{3,2,1,0:T(8,128)}, u32[]{:S(2)}) %copy-start.6) | copy-done | bytes 2097176
  130.0 3.0 %shard_map.160 = (f32[4,32,32,128]{3,2,1,0:T(8,128)}, f32[24,64,128]{2,1,0:T(8,128)}) custom-call(s32[4,2]{1,0:T(4,128)S(1)} %copy.18.corners, s32[4]{0:T(128)S(1)} %copy-done.8, f32[24]{0:T(128)S(1)} %copy-done.10, f32[4,32,32,128]{3,2,1,0:T(8,128)S(1)} %copy-done.1, f32[4,32,32,128]{3,2,1,0:T(8,128)S(1)} %copy-done.6, f32[48,88,128]{2,1,0:T(8,128)S(1)} %copy-done.2, ...), custom_call_target="tpu_custom_call" | custom-call | tf_op jit(solution)/shard_map/pallas_call | solution.py:658
  (2 shorter events, 0.0 us)
Async XLA Ops:
  1.4 1.6 %copy-start = (f32[4,32,32,128]{3,2,1,0:T(8,128)S(1)}, f32[4,32,32,128]{3,2,1,0:T(8,128)}, u32[]{:S(2)}) copy-start(f32[4,32,32,128]{3,2,1,0:T(8,128)} %eta.3) | copy-start | bytes 6291460
  3.0 0.7 copy-start.7
  3.6 0.7 copy-start.9
  5.7 1.4 %copy-start.4 = (f32[48,88,128]{2,1,0:T(8,128)}, f32[48,88,128]{2,1,0:T(8,128)S(1)}, u32[]{:S(2)}) copy-start(f32[48,88,128]{2,1,0:T(8,128)S(1)} %get-tuple-element.7.field_in) | copy-start | bytes 6488068
  7.0 1.3 copy-start.5
  8.3 116.8 %copy-start.1 = (f32[4,32,32,128]{3,2,1,0:T(8,128)S(1)}, f32[4,32,32,128]{3,2,1,0:T(8,128)}, u32[]{:S(2)}) copy-start(f32[4,32,32,128]{3,2,1,0:T(8,128)} %eta.3) | copy-start | bytes 6291460
  8.3 116.8 %copy-start.8 = (s32[4]{0:T(128)S(1)}, s32[4]{0:T(128)}, u32[]{:S(2)}) copy-start(s32[4]{0:T(128)} %ids.3) | copy-start | bytes 52
  8.3 116.8 %copy-start.10 = (f32[24]{0:T(128)S(1)}, f32[24]{0:T(128)}, u32[]{:S(2)}) copy-start(f32[24]{0:T(128)} %misfit.3) | copy-start | bytes 292
  125.2 1.6 %copy-start.2 = (f32[48,88,128]{2,1,0:T(8,128)S(1)}, f32[48,88,128]{2,1,0:T(8,128)}, u32[]{:S(2)}) copy-start(f32[48,88,128]{2,1,0:T(8,128)} %get-tuple-element.10.mu_window) | copy-start | bytes 6488068
  126.8 1.6 %copy-start.3 = (f32[48,88,128]{2,1,0:T(8,128)S(1)}, f32[48,88,128]{2,1,0:T(8,128)}, u32[]{:S(2)}) copy-start(f32[48,88,128]{2,1,0:T(8,128)} %get-tuple-element.11.oc_window) | copy-start | bytes 6488068
  128.4 1.6 %copy-start.6 = (f32[4,32,32,128]{3,2,1,0:T(8,128)S(1)}, f32[4,32,32,128]{3,2,1,0:T(8,128)}, u32[]{:S(2)}) copy-start(f32[4,32,32,128]{3,2,1,0:T(8,128)} %get-tuple-element.9.base) | copy-start | bytes 6291460

commit v4 on v3

--- a/solution.py
+++ b/solution.py
@@ -61,20 +61,13 @@
     return np.stack([np.cos(angle), np.sin(angle)]).astype(np.float32)
 
 
-def column_tables():
-    k = np.arange(NY)
-    angle = 2 * np.pi * ((k[:, None] * k[None]) % NY) / NY
-    return halves(np.concatenate([np.cos(angle), np.sin(angle)], axis=1))
-
-
-def mirror_tables():
-    rows = np.zeros((KX, KX), np.float32)
-    for j in range(1, KX):
-        rows[j, KX - j] = 1.0
-    lanes = np.zeros((NY, NY), np.float32)
-    for k in range(NY):
-        lanes[(NY - k) % NY, k] = 1.0
-    return rows.astype(jnp.bfloat16), lanes.astype(jnp.bfloat16)
+def seed_tables():
+    seeds = np.zeros((2, 104, NX), np.float32)
+    seeds[:, 0:24] = wave_rows(24, 32, NX)
+    seeds[:, 24:56] = wave_rows(32, 1, NX)
+    seeds[:, 56:72, :NY] = wave_rows(16, 32, NY)
+    seeds[:, 72:104, :NY] = wave_rows(32, 1, NY)
+    return seeds
 
 
 def split(value):
@@ -131,11 +124,9 @@
 
 
 def mega_kernel(
-    eta_in, field_in, cover_in, green_in, coarse_in, fine_in, wave_h_in, wave_l_in, back_h_in, back_l_in,
-    table_h_in, table_l_in, row_flip_in, lane_flip_in,
-    base_out, mu_out, oc_out,
-    green, coarse, fine, wave_h, wave_l, back_h, back_l, table_h, table_l, row_flip, lane_flip,
-    load_sem, eta_sem, out_sem, eta, result, field, cover, mu_window, oc_window,
+    eta, field, cover, green, seeds, waves_in,
+    result, mu_window, oc_window,
+    table_h, table_l, cut_low, cut_high, summed,
     grid, s1, r1, y1, t1, y2, t2, s2, r2, cos_h, cos_l, sin_h, sin_l,
     near, far, extra, near_row, far_row, extra_row, gs, gx, work_h, work_l, one_h, two_h, potential,
     low_y, high_y, low_x, high_x, side_o, low_o, high_o, halo_send, halo_recv, green_send, green_recv, px_send, px_recv, py_send, py_recv,
@@ -146,21 +137,7 @@
     far_from = 31 - p + upper_half - 16 * upper_half * (1 - (p + 15) // 32)
     flip, flip_row = 7 - q, (8 - q) % 8
 
-    pairs = (
-        (green_in, green), (coarse_in, coarse), (fine_in, fine), (wave_h_in, wave_h), (wave_l_in, wave_l),
-        (back_h_in, back_h), (back_l_in, back_l), (table_h_in, table_h), (table_l_in, table_l),
-        (row_flip_in, row_flip), (lane_flip_in, lane_flip),
-    )
-    boxes = eta_in.shape[0]
-    patches = [
-        pltpu.make_async_copy(field_in, field, eta_sem.at[0]),
-        pltpu.make_async_copy(cover_in, cover, eta_sem.at[1]),
-        pltpu.make_async_copy(eta_in, eta, eta_sem.at[2]),
-    ]
-    loads = [pltpu.make_async_copy(source, target, load_sem.at[n]) for n, (source, target) in enumerate(pairs)]
-    for copy in patches + loads:
-        copy.start()
-
+    boxes = eta.shape[0]
     barrier = pltpu.get_barrier_semaphore()
 
     def greet(a, b):
@@ -196,12 +173,12 @@
         return copies
 
     near_copies = [
-        push(green_in.at[3], near, green_send.at[0], green_recv.at[0], 31 - p, flip),
-        push(green_in.at[3, pl.ds(0, 8)], near_row, green_send.at[2], green_recv.at[2], 31 - p, flip_row),
+        push(green.at[3], near, green_send.at[0], green_recv.at[0], 31 - p, flip),
+        push(green.at[3, pl.ds(0, 8)], near_row, green_send.at[2], green_recv.at[2], 31 - p, flip_row),
     ]
     far_copies = [
-        push(green_in.at[2 * upper_half], far, green_send.at[1], green_recv.at[1], far_to, flip),
-        push(green_in.at[2 * upper_half, pl.ds(0, 8)], far_row, green_send.at[3], green_recv.at[3], far_to, flip_row),
+        push(green.at[2 * upper_half], far, green_send.at[1], green_recv.at[1], far_to, flip),
+        push(green.at[2 * upper_half, pl.ds(0, 8)], far_row, green_send.at[3], green_recv.at[3], far_to, flip_row),
     ]
     for copy in near_copies:
         copy.start()
@@ -213,59 +190,69 @@
         pending.append(copy)
         return copy
 
-    patches[0].wait()
     along_y = [
         halo(field.at[:, pl.ds(0, 8)], low_y, 0, p, last_q),
         halo(field.at[:, pl.ds(72, 16)], high_y, 1, p, next_q),
     ]
     for copy in along_y:
         copy.start()
-    patches[1].wait()
     side_copy = halo(cover.at[:, pl.ds(CY, OV)], side_o, 2, p, next_q)
     side_copy.start()
     for copy in along_y:
         copy.wait_recv()
-    field[:, 64:72] = field[:, 64:72] + low_y[...]
-    field[:, 8:24] = field[:, 8:24] + high_y[...]
-    along_x = [
-        halo(field.at[pl.ds(0, 12), pl.ds(8, CY)], low_x, 3, last_p, q),
-        halo(field.at[pl.ds(36, 12), pl.ds(8, CY)], high_x, 4, next_p, q),
-    ]
+
+    def joined(target, rows):
+        target[...] = field[rows, 8 : 8 + CY]
+        target[:, 0:16] = target[:, 0:16] + high_y[rows]
+        target[:, 56:64] = target[:, 56:64] + low_y[rows]
+
+    joined(cut_low, slice(0, 12))
+    joined(cut_high, slice(36, 48))
+    along_x = [halo(cut_low, low_x, 3, last_p, q), halo(cut_high, high_x, 4, next_p, q)]
     for copy in along_x:
         copy.start()
+    joined(grid, slice(12, 36))
 
     def extra_copy(a, b):
-        return push(green_in.at[0], extra, green_send.at[4], green_recv.at[4], a, b)
+        return push(green.at[0], extra, green_send.at[4], green_recv.at[4], a, b)
 
     def extra_row_copy():
-        return push(green_in.at[0, pl.ds(0, 8)], extra_row, green_send.at[5], green_recv.at[5], SPECIAL, flip_row)
+        return push(green.at[0, pl.ds(0, 8)], extra_row, green_send.at[5], green_recv.at[5], SPECIAL, flip_row)
 
     sends_extra = ((p == 0) | (p == SPECIAL)) & (q < 4)
     sends_row = (p == SPECIAL) & (q > 0) & (q < 4)
     extra_to = q + (p // SPECIAL) * (flip - q)
 
-    for copy in loads:
-        copy.wait()
-    fine_c, fine_s = fine[0], fine[1]
+    fine_c, fine_s = seeds[0, 24:56], seeds[1, 24:56]
 
     def table_body(k, unused):
-        coarse_c, coarse_s = coarse[0, pl.ds(k, 1), :], coarse[1, pl.ds(k, 1), :]
+        coarse_c, coarse_s = seeds[0, pl.ds(k, 1), :], seeds[1, pl.ds(k, 1), :]
         rows = pl.ds(pl.multiple_of(32 * k, 32), 32)
         cos_h[rows, :], cos_l[rows, :] = split(coarse_c * fine_c - coarse_s * fine_s)
         sin_h[rows, :], sin_l[rows, :] = split(coarse_s * fine_c + coarse_c * fine_s)
         return unused
 
     lax.fori_loop(0, NX // 32, table_body, 0)
+    short_c, short_s = seeds[0, 72:104, :NY], seeds[1, 72:104, :NY]
+
+    def column_body(k, unused):
+        coarse_c, coarse_s = seeds[0, pl.ds(56 + k, 1), :NY], seeds[1, pl.ds(56 + k, 1), :NY]
+        rows = pl.ds(pl.multiple_of(32 * k, 32), 32)
+        table_h[rows, 0:NY], table_l[rows, 0:NY] = split(coarse_c * short_c - coarse_s * short_s)
+        table_h[rows, NY:], table_l[rows, NY:] = split(coarse_s * short_c + coarse_c * short_s)
+        return unused
+
+    lax.fori_loop(0, NY // 32, column_body, 0)
 
     for copy in along_x:
         copy.wait_recv()
-    grid[0:12] = field[12:24, 8:72] + high_x[...]
-    grid[12:24] = field[24:36, 8:72] + low_x[...]
+    grid[0:12] = grid[0:12] + high_x[...]
+    grid[12:24] = grid[12:24] + low_x[...]
 
     keep = low_lanes((PX, 128))
     nt = (((1,), (1,)), ((), ()))
     for h in range(2):
-        waves = (wave_h[64 * h : 64 * h + 64], wave_l[64 * h : 64 * h + 64])
+        waves = (waves_in[64 * h : 64 * h + 64], waves_in[128 + 64 * h : 192 + 64 * h])
         for group in range(CX // 4):
             rows = split(grid[4 * group : 4 * group + 4].reshape(256, NZ))
             spectrum = (
@@ -302,16 +289,22 @@
         extra_row_copy().start()
 
     side_copy.wait_recv()
-    cover[:, 0:OV] = cover[:, 0:OV] + side_o[...]
+    summed[...] = cover[:, 0:CY]
+    summed[:, 0:OV] = summed[:, 0:OV] + side_o[...]
     cover_x = [
-        halo(cover.at[pl.ds(0, 24), pl.ds(0, CY)], low_o, 5, last_p, q),
-        halo(cover.at[pl.ds(24, 24), pl.ds(0, CY)], high_o, 6, next_p, q),
+        halo(summed.at[pl.ds(0, 24)], low_o, 5, last_p, q),
+        halo(summed.at[pl.ds(24, 24)], high_o, 6, next_p, q),
     ]
     for copy in cover_x:
         copy.start()
 
-    flips = row_flip[...]
-    lanes_flip = lane_flip[...]
+    def opposite(count):
+        places = lax.broadcasted_iota(jnp.int32, (count, count), 0) + lax.broadcasted_iota(jnp.int32, (count, count), 1)
+        return places, jnp.where(places == count, 1.0, 0.0)
+
+    flips = opposite(KX)[1].astype(BF16)
+    places, lanes_flip = opposite(NY)
+    lanes_flip = jnp.where(places == 0, 1.0, lanes_flip).astype(BF16)
 
     def permute(value):
         high, low = split(value)
@@ -433,8 +426,8 @@
 
     for copy in cover_x:
         copy.wait_recv()
-    oc_window[0:24, 0:CY] = cover[0:24, 0:CY] + high_o[...]
-    oc_window[24:48, 0:CY] = cover[24:48, 0:CY] + low_o[...]
+    oc_window[0:24, 0:CY] = summed[0:24] + high_o[...]
+    oc_window[24:48, 0:CY] = summed[24:48] + low_o[...]
     cover_y = halo(oc_window.at[:, pl.ds(0, OV)], oc_window.at[:, pl.ds(CY, OV)], 7, p, last_q)
     cover_y.start()
 
@@ -480,11 +473,7 @@
         r2[h, here, :] = s2[h, here, :]
 
     cover_y.wait_recv()
-    oc_copy = pltpu.make_async_copy(oc_window, oc_out, out_sem.at[boxes])
-    oc_copy.start()
-    patches[2].wait()
     sublane = lax.broadcasted_iota(jnp.int32, (32, NZ), 0)
-    outs = [oc_copy]
     for b in range(boxes):
 
         def base_body(i, unused):
@@ -501,13 +490,11 @@
             return unused
 
         lax.fori_loop(0, 32, base_body, 0, unroll=2)
-        outs.append(pltpu.make_async_copy(result.at[b], base_out.at[b], out_sem.at[b]))
-        outs[-1].start()
 
     keep = low_lanes((PX, 128))
     for h in range(2):
         drain(r2.at[h, pl.ds(0, most)], px_recv.at[1, h])
-        waves = (back_h[64 * h : 64 * h + 64], back_l[64 * h : 64 * h + 64])
+        waves = (waves_in[256 + 64 * h : 320 + 64 * h], waves_in[384 + 64 * h : 448 + 64 * h])
         for tile in range(CX // 2):
             x = 2 * tile
             even = r2.at[h][pl.ds(x, PX, stride=24), :]
@@ -524,9 +511,6 @@
     pending += around
     for copy in around:
         copy.wait_recv()
-    outs.append(pltpu.make_async_copy(mu_window, mu_out, out_sem.at[boxes + 1]))
-    outs[-1].start()
-
     for copy in pending:
         copy.wait_send()
 
@@ -543,8 +527,6 @@
         drain(s2.at[h, pl.ds(0, most)], px_send.at[1, h])
         drain(y1.at[h, pl.ds(0, PY - 1)], py_send.at[0, h])
         drain(y2.at[h, pl.ds(0, PY - 1)], py_send.at[1, h])
-    for copy in outs:
-        copy.wait()
 
 
 def place_kernel(corners, ids, misfit, eta, field, cover):
@@ -591,15 +573,12 @@
 
 def on_device(eta, corners, grain_ids, misfit, green):
     forward, inverse = depth_tables()
-    patch = pltpu.VMEM((CX + OV, CY + OV, NZ), F32)
     dma = pltpu.SemaphoreType.DMA
-    arrays = [
-        green, wave_rows(24, 32, NX), wave_rows(32, 1, NX), *halves(forward), *halves(inverse), *column_tables(),
-        *mirror_tables(),
-    ]
+    arrays = [green, seed_tables(), np.concatenate([*halves(forward), *halves(inverse)])]
     boxes = eta.shape[0]
+    vmem = pl.BlockSpec(memory_space=pltpu.VMEM)
     cells = shaped(CX + OV, CY + OV, NZ)
-    local = pltpu.CompilerParams(vmem_limit_bytes=32 * 1024 * 1024)
+    local = pltpu.CompilerParams(vmem_limit_bytes=24 * 1024 * 1024)
     field, cover = pl.pallas_call(
         place_kernel,
         out_shape=[cells, cells],
@@ -608,13 +587,11 @@
         compiler_params=local,
     )(corners, grain_ids, misfit, eta)
     scratch = [
-        *[pltpu.VMEM(a.shape, a.dtype) for a in arrays],
-        dma((len(arrays),)),
-        dma((3,)),
-        dma((boxes + 2,)),
-        pltpu.VMEM((boxes, 32, 32, NZ), F32),
-        pltpu.VMEM((boxes, 32, 32, NZ), F32),
-        *[patch] * 4,
+        pltpu.VMEM((NY, 2 * NY), BF16),
+        pltpu.VMEM((NY, 2 * NY), BF16),
+        pltpu.VMEM((12, CY, NZ), F32),
+        pltpu.VMEM((12, CY, NZ), F32),
+        pltpu.VMEM((CX + OV, CY, NZ), F32),
         pltpu.VMEM((CX, CY, NZ), F32),
         pltpu.VMEM((2, NX, 128), F32),
         pltpu.VMEM((2, NX, 128), F32),
@@ -642,15 +619,14 @@
         dma((6,)),
         *[dma((2, 2))] * 4,
     ]
-    hbm = pl.BlockSpec(memory_space=pl.ANY)
     base, mu, total = pl.pallas_call(
         mega_kernel,
         out_shape=[shaped(*eta.shape), cells, cells],
-        in_specs=[hbm] * (3 + len(arrays)),
-        out_specs=[hbm] * 3,
+        in_specs=[vmem] * (3 + len(arrays)),
+        out_specs=[vmem] * 3,
         scratch_shapes=scratch,
         compiler_params=pltpu.CompilerParams(
-            vmem_limit_bytes=56 * 1024 * 1024, collective_id=0, has_side_effects=True
+            vmem_limit_bytes=36 * 1024 * 1024, collective_id=0, has_side_effects=True
         ),
     )(eta, field, cover, *arrays)
     block = pl.BlockSpec((1, 32, 32, NZ), lambda b: (b, 0, 0, 0))

time: 134 us -> 128 us (0.955)
  local copies, waits for them, and re-layouts: 11.2 us -> 7.04 us
    unnamed x23 -> x19, local copies, waits for them, and re-layouts: 11.2 us -> 7.04 us
where the time goes in v4:
time: 128 us
  Pallas kernels  120 us (94%)
  local copies, waits for them, and re-layouts  7.04 us (6%)
    pallas_call x1, Pallas kernels, on_device(): pl.pallas_call(mega_kernel, out_shape=[shaped(*eta.shape), cells, cells],...  116 us
    unnamed x19, local copies, waits for them, and re-layouts  7.04 us
    pallas_call x1, Pallas kernels, on_device(): pl.pallas_call(final_kernel, grid=(boxes,), out_shape=[shaped(*eta.shape)...  3.06 us

profile of v4, /device:TPU:1, one launch (start us, length us, event | category | flops | bytes accessed | tf_op | source)
XLA Modules:
  0.0 127.6 jit_solution(11762726145126858737)
XLA Ops:
  0.6 0.8 copy.10.corners
  1.4 0.0 copy-start
  1.4 1.6 %copy-done = f32[4,32,32,128]{3,2,1,0:T(8,128)S(1)} copy-done((f32[4,32,32,128]{3,2,1,0:T(8,128)S(1)}, f32[4,32,32,128]{3,2,1,0:T(8,128)}, u32[]{:S(2)}) %copy-start) | copy-done | bytes 2097176
  3.0 0.0 copy-start.5
  3.0 0.7 copy-done.5
  3.6 0.0 copy-start.7
  3.6 0.7 copy-done.7
  4.3 0.0 copy-start.1
  4.3 1.3 %shard_map.86 = (f32[48,88,128]{2,1,0:T(8,128)S(1)}, f32[48,88,128]{2,1,0:T(8,128)S(1)}) custom-call(s32[4,2]{1,0:T(4,128)S(1)} %copy.10.corners, s32[4]{0:T(128)S(1)} %copy-done.5, f32[24]{0:T(128)S(1)} %copy-done.7, f32[4,32,32,128]{3,2,1,0:T(8,128)S(1)} %copy-done), custom_call_target="tpu_custom_call" | custom-call | tf_op jit(solution)/shard_map/pallas_call | solution.py:582
  5.6 0.3 copy-done.1
  5.9 0.0 copy-start.2
  5.9 1.1 copy-done.2
  7.0 0.0 copy-start.3
  7.0 1.1 copy-done.3
  8.1 0.0 copy-start.4
  8.1 0.9 copy-done.4
  9.0 0.0 copy-start.6
  9.0 0.0 copy-start.8
  9.0 115.5 %shard_map.87 = (f32[4,32,32,128]{3,2,1,0:T(8,128)S(1)}, f32[48,88,128]{2,1,0:T(8,128)S(1)}, f32[48,88,128]{2,1,0:T(8,128)S(1)}) custom-call(f32[4,32,32,128]{3,2,1,0:T(8,128)S(1)} %copy-done.1, f32[48,88,128]{2,1,0:T(8,128)S(1)} %get-tuple-element.7.field, f32[48,88,128]{2,1,0:T(8,128)S(1)} %get-tuple-element.8.cover, f32[4,96,512]{2,1,0:T(8,128)S(1)} %copy-done.2, ...), custom_call_target="tpu_custom_call" | custom-call | tf_op jit(solution)/shard_map/pallas_call | solution.py:622
  124.5 0.0 copy-done.6
  124.6 0.0 copy-done.8
  124.6 3.1 %shard_map.88 = (f32[4,32,32,128]{3,2,1,0:T(8,128)}, f32[24,64,128]{2,1,0:T(8,128)}) custom-call(s32[4,2]{1,0:T(4,128)S(1)} %copy.10.corners, s32[4]{0:T(128)S(1)} %copy-done.6, f32[24]{0:T(128)S(1)} %copy-done.8, f32[4,32,32,128]{3,2,1,0:T(8,128)S(1)} %copy-done.1, f32[4,32,32,128]{3,2,1,0:T(8,128)S(1)} %get-tuple-element.9.base, ...), custom_call_target="tpu_custom_call" | custom-call | tf_op jit(solution)/shard_map/pallas_call | solution.py:634
Async XLA Ops:
  1.4 1.6 %copy-start = (f32[4,32,32,128]{3,2,1,0:T(8,128)S(1)}, f32[4,32,32,128]{3,2,1,0:T(8,128)}, u32[]{:S(2)}) copy-start(f32[4,32,32,128]{3,2,1,0:T(8,128)} %eta.5) | copy-start | bytes 6291460
  3.0 0.7 copy-start.5
  3.6 0.7 copy-start.7
  4.3 1.6 %copy-start.1 = (f32[4,32,32,128]{3,2,1,0:T(8,128)S(1)}, f32[4,32,32,128]{3,2,1,0:T(8,128)}, u32[]{:S(2)}) copy-start(f32[4,32,32,128]{3,2,1,0:T(8,128)} %eta.5) | copy-start | bytes 6291460
  5.9 1.1 copy-start.2
  7.0 1.1 copy-start.3
  8.1 0.9 copy-start.4
  9.0 115.5 %copy-start.6 = (s32[4]{0:T(128)S(1)}, s32[4]{0:T(128)}, u32[]{:S(2)}) copy-start(s32[4]{0:T(128)} %ids.3) | copy-start | bytes 52
  9.0 115.5 %copy-start.8 = (f32[24]{0:T(128)S(1)}, f32[24]{0:T(128)}, u32[]{:S(2)}) copy-start(f32[24]{0:T(128)} %misfit.3) | copy-start | bytes 292

commit v5 on v4

--- a/solution.py
+++ b/solution.py
@@ -383,9 +383,29 @@
         gs[1] = jnp.where(top, jnp.broadcast_to(packed_rows[0:1], (KX, NY)), half)
         gx[...] = packed_rows[8:16]
 
+    def base_update():
+        sublane = lax.broadcasted_iota(jnp.int32, (32, NZ), 0)
+        for b in range(boxes):
+
+            def base_body(i, unused):
+                value = eta[b, i]
+                before = jnp.where(i > 0, eta[b, jnp.maximum(i - 1, 0)], 0.0)
+                after = jnp.where(i < 31, eta[b, jnp.minimum(i + 1, 31)], 0.0)
+                above = jnp.where(sublane == 0, 0.0, pltpu.roll(value, 1, axis=0))
+                below = jnp.where(sublane == 31, 0.0, pltpu.roll(value, 31, axis=0))
+                lap = before + after + above + below + pltpu.roll(value, 1, axis=1) + pltpu.roll(value, 127, axis=1)
+                lap = lap - 6.0 * value
+                square = value * value
+                force = value * square - value - 2.0 * COUPLING * value * square - GRADIENT * lap
+                result[b, i] = value - RATE * force
+                return unused
+
+            lax.fori_loop(0, 32, base_body, 0, unroll=2)
+
     tables = (table_h[...], table_l[...])
     for h in range(2):
         if h == 1:
+            base_update()
             second_green()
         drain(t1.at[h, pl.ds(0, PY - 1)], py_recv.at[0, h])
         for tile in range(4):
@@ -472,25 +492,6 @@
         here = pl.ds(pl.multiple_of(24 * p, 8), 24)
         r2[h, here, :] = s2[h, here, :]
 
-    cover_y.wait_recv()
-    sublane = lax.broadcasted_iota(jnp.int32, (32, NZ), 0)
-    for b in range(boxes):
-
-        def base_body(i, unused):
-            value = eta[b, i]
-            before = jnp.where(i > 0, eta[b, jnp.maximum(i - 1, 0)], 0.0)
-            after = jnp.where(i < 31, eta[b, jnp.minimum(i + 1, 31)], 0.0)
-            above = jnp.where(sublane == 0, 0.0, pltpu.roll(value, 1, axis=0))
-            below = jnp.where(sublane == 31, 0.0, pltpu.roll(value, 31, axis=0))
-            lap = before + after + above + below + pltpu.roll(value, 1, axis=1) + pltpu.roll(value, 127, axis=1)
-            lap = lap - 6.0 * value
-            square = value * value
-            force = value * square - value - 2.0 * COUPLING * value * square - GRADIENT * lap
-            result[b, i] = value - RATE * force
-            return unused
-
-        lax.fori_loop(0, 32, base_body, 0, unroll=2)
-
     keep = low_lanes((PX, 128))
     for h in range(2):
         drain(r2.at[h, pl.ds(0, most)], px_recv.at[1, h])
@@ -509,7 +510,7 @@
 
     around = spread(potential, mu_window, 1)
     pending += around
-    for copy in around:
+    for copy in around + [cover_y]:
         copy.wait_recv()
     for copy in pending:
         copy.wait_send()

time: 128 us -> 128 us (level)
  no operation moved by 1% of the time
where the time goes in v5:
time: 128 us
  Pallas kernels  120 us (94%)
  local copies, waits for them, and re-layouts  7 us (5%)
    pallas_call x1, Pallas kernels, on_device(): pl.pallas_call(mega_kernel, out_shape=[shaped(*eta.shape), cells, cells],...  116 us
    unnamed x19, local copies, waits for them, and re-layouts  7 us
    pallas_call x1, Pallas kernels, on_device(): pl.pallas_call(final_kernel, grid=(boxes,), out_shape=[shaped(*eta.shape)...  3.1 us

profile of v5, /device:TPU:1, one launch (start us, length us, event | category | flops | bytes accessed | tf_op | source)
XLA Modules:
  0.0 127.8 jit_solution(10917281708748017721)
XLA Ops:
  0.6 0.8 copy.10.corners
  1.4 0.0 copy-start
  1.4 1.6 %copy-done = f32[4,32,32,128]{3,2,1,0:T(8,128)S(1)} copy-done((f32[4,32,32,128]{3,2,1,0:T(8,128)S(1)}, f32[4,32,32,128]{3,2,1,0:T(8,128)}, u32[]{:S(2)}) %copy-start) | copy-done | bytes 2097176
  3.0 0.0 copy-start.5
  3.0 0.7 copy-done.5
  3.6 0.0 copy-start.7
  3.6 0.7 copy-done.7
  4.3 0.0 copy-start.1
  4.3 1.4 %shard_map.86 = (f32[48,88,128]{2,1,0:T(8,128)S(1)}, f32[48,88,128]{2,1,0:T(8,128)S(1)}) custom-call(s32[4,2]{1,0:T(4,128)S(1)} %copy.10.corners, s32[4]{0:T(128)S(1)} %copy-done.5, f32[24]{0:T(128)S(1)} %copy-done.7, f32[4,32,32,128]{3,2,1,0:T(8,128)S(1)} %copy-done), custom_call_target="tpu_custom_call" | custom-call | tf_op jit(solution)/shard_map/pallas_call | solution.py:583
  5.7 0.2 copy-done.1
  5.9 0.0 copy-start.2
  5.9 1.1 copy-done.2
  7.0 0.0 copy-start.3
  7.0 1.1 copy-done.3
  8.1 0.0 copy-start.4
  8.1 0.9 copy-done.4
  9.0 0.0 copy-start.6
  9.0 0.0 copy-start.8
  9.0 115.6 %shard_map.87 = (f32[4,32,32,128]{3,2,1,0:T(8,128)S(1)}, f32[48,88,128]{2,1,0:T(8,128)S(1)}, f32[48,88,128]{2,1,0:T(8,128)S(1)}) custom-call(f32[4,32,32,128]{3,2,1,0:T(8,128)S(1)} %copy-done.1, f32[48,88,128]{2,1,0:T(8,128)S(1)} %get-tuple-element.7.field, f32[48,88,128]{2,1,0:T(8,128)S(1)} %get-tuple-element.8.cover, f32[4,96,512]{2,1,0:T(8,128)S(1)} %copy-done.2, ...), custom_call_target="tpu_custom_call" | custom-call | tf_op jit(solution)/shard_map/pallas_call | solution.py:623
  124.7 0.0 copy-done.6
  124.7 0.0 copy-done.8
  124.7 3.1 %shard_map.88 = (f32[4,32,32,128]{3,2,1,0:T(8,128)}, f32[24,64,128]{2,1,0:T(8,128)}) custom-call(s32[4,2]{1,0:T(4,128)S(1)} %copy.10.corners, s32[4]{0:T(128)S(1)} %copy-done.6, f32[24]{0:T(128)S(1)} %copy-done.8, f32[4,32,32,128]{3,2,1,0:T(8,128)S(1)} %copy-done.1, f32[4,32,32,128]{3,2,1,0:T(8,128)S(1)} %get-tuple-element.9.base, ...), custom_call_target="tpu_custom_call" | custom-call | tf_op jit(solution)/shard_map/pallas_call | solution.py:635
Async XLA Ops:
  1.4 1.6 %copy-start = (f32[4,32,32,128]{3,2,1,0:T(8,128)S(1)}, f32[4,32,32,128]{3,2,1,0:T(8,128)}, u32[]{:S(2)}) copy-start(f32[4,32,32,128]{3,2,1,0:T(8,128)} %eta.5) | copy-start | bytes 6291460
  3.0 0.7 copy-start.5
  3.6 0.7 copy-start.7
  4.3 1.6 %copy-start.1 = (f32[4,32,32,128]{3,2,1,0:T(8,128)S(1)}, f32[4,32,32,128]{3,2,1,0:T(8,128)}, u32[]{:S(2)}) copy-start(f32[4,32,32,128]{3,2,1,0:T(8,128)} %eta.5) | copy-start | bytes 6291460
  5.9 1.1 copy-start.2
  7.0 1.1 copy-start.3
  8.1 0.9 copy-start.4
  9.0 115.7 %copy-start.6 = (s32[4]{0:T(128)S(1)}, s32[4]{0:T(128)}, u32[]{:S(2)}) copy-start(s32[4]{0:T(128)} %ids.3) | copy-start | bytes 52
  9.0 115.7 %copy-start.8 = (f32[24]{0:T(128)S(1)}, f32[24]{0:T(128)}, u32[]{:S(2)}) copy-start(f32[24]{0:T(128)} %misfit.3) | copy-start | bytes 292

commit v6 on v4

--- a/solution.py
+++ b/solution.py
@@ -249,6 +249,16 @@
     grid[0:12] = grid[0:12] + high_x[...]
     grid[12:24] = grid[12:24] + low_x[...]
 
+    side_copy.wait_recv()
+    summed[...] = cover[:, 0:CY]
+    summed[:, 0:OV] = summed[:, 0:OV] + side_o[...]
+    cover_x = [
+        halo(summed.at[pl.ds(0, 24)], low_o, 5, last_p, q),
+        halo(summed.at[pl.ds(24, 24)], high_o, 6, next_p, q),
+    ]
+    for copy in cover_x:
+        copy.start()
+
     keep = low_lanes((PX, 128))
     nt = (((1,), (1,)), ((), ()))
     for h in range(2):
@@ -287,16 +297,6 @@
     @pl.when(sends_row)
     def _():
         extra_row_copy().start()
-
-    side_copy.wait_recv()
-    summed[...] = cover[:, 0:CY]
-    summed[:, 0:OV] = summed[:, 0:OV] + side_o[...]
-    cover_x = [
-        halo(summed.at[pl.ds(0, 24)], low_o, 5, last_p, q),
-        halo(summed.at[pl.ds(24, 24)], high_o, 6, next_p, q),
-    ]
-    for copy in cover_x:
-        copy.start()
 
     def opposite(count):
         places = lax.broadcasted_iota(jnp.int32, (count, count), 0) + lax.broadcasted_iota(jnp.int32, (count, count), 1)

time: 128 us -> 144 us (1.12)
  Pallas kernels: 120 us -> 136 us
    pallas_call x1, Pallas kernels: 116 us -> 132 us  [on_device(): pl.pallas_call(mega_kernel, out_shape=[shaped(*eta.shape), cells, cells],...]
where the time goes in v6:
time: 144 us
  Pallas kernels  136 us (94%)
  local copies, waits for them, and re-layouts  7.03 us (5%)
    pallas_call x1, Pallas kernels, on_device(): pl.pallas_call(mega_kernel, out_shape=[shaped(*eta.shape), cells, cells],...  132 us
    unnamed x19, local copies, waits for them, and re-layouts  7.03 us
    pallas_call x1, Pallas kernels, on_device(): pl.pallas_call(final_kernel, grid=(boxes,), out_shape=[shaped(*eta.shape)...  3.08 us

profile of v6, /device:TPU:1, one launch (start us, length us, event | category | flops | bytes accessed | tf_op | source)
XLA Modules:
  0.0 143.8 jit_solution(14754984203242121850)
XLA Ops:
  0.6 0.8 copy.10.corners
  1.4 0.0 copy-start
  1.4 1.6 %copy-done = f32[4,32,32,128]{3,2,1,0:T(8,128)S(1)} copy-done((f32[4,32,32,128]{3,2,1,0:T(8,128)S(1)}, f32[4,32,32,128]{3,2,1,0:T(8,128)}, u32[]{:S(2)}) %copy-start) | copy-done | bytes 2097176
  3.0 0.0 copy-start.5
  3.0 0.7 copy-done.5
  3.6 0.0 copy-start.7
  3.6 0.7 copy-done.7
  4.3 0.0 copy-start.1
  4.3 1.4 shard_map.86
  5.7 0.2 copy-done.1
  5.9 0.0 copy-start.2
  5.9 1.1 copy-done.2
  7.0 0.0 copy-start.3
  7.0 1.1 copy-done.3
  8.1 0.0 copy-start.4
  8.1 0.9 copy-done.4
  9.0 0.0 copy-start.6
  9.0 0.0 copy-start.8
  9.0 131.7 %shard_map.87 = (f32[4,32,32,128]{3,2,1,0:T(8,128)S(1)}, f32[48,88,128]{2,1,0:T(8,128)S(1)}, f32[48,88,128]{2,1,0:T(8,128)S(1)}) custom-call(f32[4,32,32,128]{3,2,1,0:T(8,128)S(1)} %copy-done.1, f32[48,88,128]{2,1,0:T(8,128)S(1)} %get-tuple-element.7.field, f32[48,88,128]{2,1,0:T(8,128)S(1)} %get-tuple-element.8.cover, f32[4,96,512]{2,1,0:T(8,128)S(1)} %copy-done.2, ...), custom_call_target="tpu_custom_call" | custom-call | tf_op jit(solution)/shard_map/pallas_call | solution.py:622
  140.7 0.0 copy-done.6
  140.7 0.0 copy-done.8
  140.7 3.1 %shard_map.88 = (f32[4,32,32,128]{3,2,1,0:T(8,128)}, f32[24,64,128]{2,1,0:T(8,128)}) custom-call(s32[4,2]{1,0:T(4,128)S(1)} %copy.10.corners, s32[4]{0:T(128)S(1)} %copy-done.6, f32[24]{0:T(128)S(1)} %copy-done.8, f32[4,32,32,128]{3,2,1,0:T(8,128)S(1)} %copy-done.1, f32[4,32,32,128]{3,2,1,0:T(8,128)S(1)} %get-tuple-element.9.base, ...), custom_call_target="tpu_custom_call" | custom-call | tf_op jit(solution)/shard_map/pallas_call | solution.py:634
Async XLA Ops:
  1.4 1.6 %copy-start = (f32[4,32,32,128]{3,2,1,0:T(8,128)S(1)}, f32[4,32,32,128]{3,2,1,0:T(8,128)}, u32[]{:S(2)}) copy-start(f32[4,32,32,128]{3,2,1,0:T(8,128)} %eta.5) | copy-start | bytes 6291460
  3.0 0.7 copy-start.5
  3.6 0.7 copy-start.7
  4.3 1.6 %copy-start.1 = (f32[4,32,32,128]{3,2,1,0:T(8,128)S(1)}, f32[4,32,32,128]{3,2,1,0:T(8,128)}, u32[]{:S(2)}) copy-start(f32[4,32,32,128]{3,2,1,0:T(8,128)} %eta.5) | copy-start | bytes 6291460
  5.9 1.1 copy-start.2
  7.0 1.1 copy-start.3
  8.1 0.9 copy-start.4
  9.0 131.7 %copy-start.6 = (s32[4]{0:T(128)S(1)}, s32[4]{0:T(128)}, u32[]{:S(2)}) copy-start(s32[4]{0:T(128)} %ids.3) | copy-start | bytes 52
  9.0 131.7 %copy-start.8 = (f32[24]{0:T(128)S(1)}, f32[24]{0:T(128)}, u32[]{:S(2)}) copy-start(f32[24]{0:T(128)} %misfit.3) | copy-start | bytes 292
